TPU v7x, 32 devices: a whole 2x2x4 slice. The times are simulated.
32 devices in a mesh: fsdp: 8 (over y, x, core), mp: 4 (over z).
Axes of the slice: x: 2, y: 2, z: 4, core: 2. Of those that a mesh axis runs over, the one named last changes fastest.
Arguments:
- layer_input: float32 [4096, 768], P(('fsdp', 'mp')), may hold values from -6 to 6
- cotangent: float32 [4096, 768], P(('fsdp', 'mp')), may hold values from -6 to 6
- seq_lengths: int32 [4], replicated, may hold values from 1 to 2048, 4096 in all
- gain_attn: bfloat16 [768], P('fsdp'), may hold values from 0.5 to 1.5
- beta_attn: bfloat16 [768], P('fsdp'), may hold values from -3 to 3
- gain_mlp: bfloat16 [768], P('fsdp'), may hold values from 0.5 to 1.5
- beta_mlp: bfloat16 [768], P('fsdp'), may hold values from -3 to 3
- qkv_weight: bfloat16 [768, 3, 12, 64], P('fsdp'), may hold values from -0.21875 to 0.21875
- qkv_bias: bfloat16 [2304], P('fsdp'), may hold values from -3 to 3
- dense_weight: bfloat16 [768, 768], P(None, 'fsdp'), may hold values from -0.875 to 0.875
- dense_bias: bfloat16 [768], P('fsdp'), may hold values from -3 to 3
- up_weight: bfloat16 [768, 3072], P('fsdp', 'mp'), may hold values from -0.21875 to 0.21875
- up_bias: bfloat16 [3072], P('fsdp'), may hold values from -3 to 3
- down_weight: bfloat16 [768, 3072], P('fsdp', 'mp'), may hold values from -0.15625 to 0.15625
- down_bias: bfloat16 [768], P('fsdp'), may hold values from -3 to 3
Outputs:
- layer_output: float32 [4096, 768], P(('fsdp', 'mp'))
- input_grad: float32 [4096, 768], P(('fsdp', 'mp'))
- grad_qkv_weight: float32 [768, 3, 12, 64], P('fsdp')
- grad_qkv_bias: float32 [2304], P('fsdp')
- grad_dense_weight: float32 [768, 768], P(None, 'fsdp')
- grad_dense_bias: float32 [768], P('fsdp')
- grad_gain_attn: float32 [768], P('fsdp')
- grad_beta_attn: float32 [768], P('fsdp')
- grad_gain_mlp: float32 [768], P('fsdp')
- grad_beta_mlp: float32 [768], P('fsdp')
- grad_up_weight: float32 [768, 3072], P('fsdp', 'mp')
- grad_up_bias: float32 [3072], P('fsdp')
- grad_down_weight: float32 [768, 3072], P('fsdp', 'mp')
- grad_down_bias: float32 [768], P('fsdp')
Inputs may be any that keep to these rules, and one draw needn't show every extreme that they name: `seq_lengths`: the longest sequence has exactly 2048 tokens; all lengths sum to 4096.
All inputs are finite; a program needn't handle non-finite values.
Results may differ from a plain program's by a relative error of at most 0.013.
Values may be sent and summed in bfloat16 or wider, within the bound.
A program may use at most 192 MiB of HBM per device.

v0:
```python
import math

import jax
import jax.numpy as jnp
from jax import lax
from jax.sharding import PartitionSpec as P

ROT = 16
SPAN = 16


EPS = 1e-05
NEG_FILL = -1e30


def from_behind(value, axis, steps):
    count = lax.axis_size(axis)
    initial, last = (max(0, -steps), min(count, count - steps))
    return lax.ppermute(value, axis, [(source, source + steps) for source in range(initial, last)])


def norm_parts(inputs):
    row_mean = jnp.mean(inputs, axis=-1, keepdims=True)
    centred = inputs - row_mean
    row_var = jnp.mean(centred * centred, axis=-1, keepdims=True)
    inv_std = lax.rsqrt(row_var + EPS)
    return (centred * inv_std, inv_std)


def norm_back(grad_hat, normed, inv_std):
    first_mean = jnp.mean(grad_hat, axis=-1, keepdims=True)
    second_mean = jnp.mean(grad_hat * normed, axis=-1, keepdims=True)
    return inv_std * (grad_hat - first_mean - normed * second_mean)


def gelu_value(pre_act):
    return 0.5 * pre_act * (1.0 + lax.erf(pre_act * (1.0 / math.sqrt(2.0))))


def gelu_slope(pre_act):
    cumulative = 0.5 * (1.0 + lax.erf(pre_act * (1.0 / math.sqrt(2.0))))
    return cumulative + pre_act * jnp.exp(-0.5 * pre_act * pre_act) * (
        1.0 / math.sqrt(2.0 * math.pi)
    )


def rotary_tables(positions):
    half_rot = ROT // 2
    inverse = jnp.exp(jnp.arange(half_rot, dtype=jnp.float32) * (-2.0 * math.log(10000.0) / ROT))
    phase_angle = positions.astype(jnp.float32)[:, None] * inverse[None, :]
    return (jnp.cos(phase_angle)[:, None, :], jnp.sin(phase_angle)[:, None, :])


def rotate(vectors, cosine, sine_table):
    half_rot = ROT // 2
    first_half = vectors[..., :half_rot]
    second_half = vectors[..., half_rot:ROT]
    return jnp.concatenate(
        [
            first_half * cosine - second_half * sine_table,
            second_half * cosine + first_half * sine_table,
            vectors[..., ROT:],
        ],
        axis=-1,
    )


def rotate_back(grads, cosine, sine_table):
    half_rot = ROT // 2
    first_half = grads[..., :half_rot]
    second_half = grads[..., half_rot:ROT]
    return jnp.concatenate(
        [
            first_half * cosine + second_half * sine_table,
            second_half * cosine - first_half * sine_table,
            grads[..., ROT:],
        ],
        axis=-1,
    )


def token_segments(seq_lengths, token_index):
    seq_ends = jnp.cumsum(seq_lengths, dtype=jnp.int32)
    seq_starts = seq_ends - seq_lengths
    segment_ids = jnp.sum(
        (seq_ends[None, :] <= token_index[:, None]).astype(jnp.int32), axis=1, dtype=jnp.int32
    )
    chosen = segment_ids[:, None] == jnp.arange(seq_lengths.shape[0], dtype=jnp.int32)[None, :]
    first_token = jnp.sum(jnp.where(chosen, seq_starts[None, :], 0), axis=1, dtype=jnp.int32)
    return (segment_ids, token_index - first_token)


def contract_rows(left, right):
    return lax.dot_general(
        left, right, (((0,), (0,)), ((), ())), preferred_element_type=jnp.float32
    )


def contract_cols(left, right):
    return lax.dot_general(
        left, right, (((1,), (1,)), ((), ())), preferred_element_type=jnp.float32
    )


def on_device(
    layer_input,
    cotangent,
    seq_lengths,
    gain_attn,
    beta_attn,
    gain_mlp,
    beta_mlp,
    qkv_weight,
    qkv_bias,
    dense_weight,
    dense_bias,
    up_weight,
    up_bias,
    down_weight,
    down_bias,
):
    fsdp_count = lax.axis_size("fsdp")
    model_count = lax.axis_size("mp")
    fsdp_rank = lax.axis_index("fsdp")
    model_rank = lax.axis_index("mp")
    tok_dev = layer_input.shape[0]
    model_width = layer_input.shape[1]
    head_count = qkv_weight.shape[2]
    head_dim = qkv_weight.shape[3]
    local_heads = head_count // model_count
    local_width = local_heads * head_dim
    group_rows = model_count * tok_dev
    key_reach = min(SPAN * group_rows, group_rows * fsdp_count // 2)
    hop_total = key_reach // group_rows
    score_scale = 1.0 / math.sqrt(head_dim)
    (
        full_qkv,
        full_dense_t,
        full_up,
        full_down,
        full_qkv_bias,
        full_dense_bias,
        full_up_bias,
        full_down_bias,
        full_gain_attn,
        full_beta_attn,
        full_gain_mlp,
        full_beta_mlp,
    ) = (
        lax.all_gather(qkv_weight, "fsdp", axis=0, tiled=True),
        lax.all_gather(dense_weight.T, "fsdp", axis=0, tiled=True),
        lax.all_gather(up_weight, "fsdp", axis=0, tiled=True),
        lax.all_gather(down_weight, "fsdp", axis=0, tiled=True),
        lax.all_gather(qkv_bias, "fsdp", axis=0, tiled=True),
        lax.all_gather(dense_bias, "fsdp", axis=0, tiled=True),
        lax.all_gather(up_bias, "fsdp", axis=0, tiled=True),
        lax.all_gather(down_bias, "fsdp", axis=0, tiled=True),
        lax.all_gather(gain_attn, "fsdp", axis=0, tiled=True),
        lax.all_gather(beta_attn, "fsdp", axis=0, tiled=True),
        lax.all_gather(gain_mlp, "fsdp", axis=0, tiled=True),
        lax.all_gather(beta_mlp, "fsdp", axis=0, tiled=True),
    )
    hidden_local = full_up.shape[1]
    w_qkv = full_qkv.reshape(model_width, 3 * model_width)
    dense_local = lax.dynamic_slice_in_dim(full_dense_t, model_rank * local_width, local_width, 1)
    gain_one = full_gain_attn.astype(jnp.float32)
    gain_two = full_gain_mlp.astype(jnp.float32)
    up_bias_local = lax.dynamic_slice_in_dim(
        full_up_bias, model_rank * hidden_local, hidden_local, 0
    ).astype(jnp.float32)
    group_index = fsdp_rank * group_rows + jnp.arange(group_rows, dtype=jnp.int32)
    group_seg, group_pos = token_segments(seq_lengths, group_index)
    group_cos, group_sin = rotary_tables(group_pos)
    causal_mask = (
        jnp.arange(group_rows, dtype=jnp.int32)[None, :]
        <= jnp.arange(group_rows, dtype=jnp.int32)[:, None]
    )
    normed, inv_std = norm_parts(layer_input)
    h_attn = (normed * gain_one + full_beta_attn.astype(jnp.float32)).astype(jnp.bfloat16)
    h_mlp = (normed * gain_two + full_beta_mlp.astype(jnp.float32)).astype(jnp.bfloat16)
    own_index = (fsdp_rank * model_count + model_rank) * tok_dev + jnp.arange(
        tok_dev, dtype=jnp.int32
    )
    unused_seg, own_pos = token_segments(seq_lengths, own_index)
    own_cos, own_sin = rotary_tables(own_pos)
    projected = (
        jnp.dot(h_attn, w_qkv, preferred_element_type=jnp.float32)
        + full_qkv_bias.astype(jnp.float32)[None, :]
    )
    projected = projected.reshape(tok_dev, 3, head_count, head_dim)
    stacked = jnp.stack(
        [
            rotate(projected[:, 0], own_cos, own_sin),
            rotate(projected[:, 1], own_cos, own_sin),
            projected[:, 2],
        ],
        axis=1,
    )
    stacked = stacked.astype(jnp.bfloat16).reshape(tok_dev, 3, head_count * head_dim)
    heads_local = lax.all_to_all(stacked, "mp", split_axis=2, concat_axis=0, tiled=True)
    mlp_rows = lax.all_gather(h_mlp, "mp", axis=0, tiled=True)
    query_rows = heads_local[:, 0].reshape(group_rows, local_heads, head_dim)
    own_pair = heads_local[:, 1:]
    key_sets = []
    moving = own_pair
    for distance in range(1, hop_total + 1):
        moving = from_behind(moving, "fsdp", 1)
        earlier_index = group_index - distance * group_rows
        earlier_seg, unused_pos = token_segments(seq_lengths, earlier_index)
        earlier_seg = jnp.where(earlier_index >= 0, earlier_seg, -1)
        key_sets.append((moving, earlier_seg, distance))

    def is_live(key_segs):
        return key_segs[-1] == group_seg[0]

    def block_scores(pair, key_segs, causal):
        key_block = pair[:, 0].reshape(group_rows, local_heads, head_dim)
        scores = (
            jnp.einsum("qhd,khd->hqk", query_rows, key_block, preferred_element_type=jnp.float32)
            * score_scale
        )
        key_mask = group_seg[:, None] == key_segs[None, :]
        if causal:
            key_mask = key_mask & causal_mask
        return (scores, key_mask[None])

    def stats_update(carried_state, pair, key_segs):
        row_top, row_total = carried_state
        scores, key_mask = block_scores(pair, key_segs, False)
        masked = jnp.where(key_mask, scores, NEG_FILL)
        new_top = jnp.maximum(row_top, jnp.max(masked, axis=-1))
        new_total = row_total * jnp.exp(row_top - new_top) + jnp.sum(
            jnp.where(key_mask, jnp.exp(masked - new_top[..., None]), 0.0), axis=-1
        )
        return (new_top, new_total)

    scores, key_mask = block_scores(own_pair, group_seg, True)
    masked = jnp.where(key_mask, scores, NEG_FILL)
    row_top = jnp.max(masked, axis=-1)
    row_total = jnp.sum(jnp.where(key_mask, jnp.exp(masked - row_top[..., None]), 0.0), axis=-1)
    for pair, key_segs, distance in key_sets:
        row_top, row_total = lax.cond(
            is_live(key_segs),
            lambda carried_state: stats_update(carried_state, pair, key_segs),
            lambda carried_state: carried_state,
            (row_top, row_total),
        )
    row_lse = row_top + jnp.log(row_total)

    def block_output(pair, key_segs, causal):
        scores, key_mask = block_scores(pair, key_segs, causal)
        attn_probs = jnp.where(key_mask, jnp.exp(scores - row_lse[..., None]), 0.0).astype(
            jnp.bfloat16
        )
        value_block = pair[:, 1].reshape(group_rows, local_heads, head_dim)
        return jnp.einsum(
            "hqk,khd->qhd", attn_probs, value_block, preferred_element_type=jnp.float32
        )

    zero_heads = jnp.zeros((group_rows, local_heads, head_dim), jnp.float32)
    mixed = block_output(own_pair, group_seg, True)
    for pair, key_segs, distance in key_sets:
        mixed = mixed + lax.cond(
            is_live(key_segs), lambda: block_output(pair, key_segs, False), lambda: zero_heads
        )
    out_heads = mixed.astype(jnp.bfloat16)
    out_flat = out_heads.reshape(group_rows, local_width)
    attn_heads = lax.all_to_all(out_flat, "mp", split_axis=0, concat_axis=1, tiled=True)
    attn_out = (
        contract_cols(attn_heads, full_dense_t) + full_dense_bias.astype(jnp.float32)[None, :]
    )
    pre_act = (
        jnp.dot(mlp_rows, full_up, preferred_element_type=jnp.float32) + up_bias_local[None, :]
    )
    activation = gelu_value(pre_act).astype(jnp.bfloat16)
    row_part = activation
    terms = contract_cols(row_part, full_down)
    branch_sum = lax.psum_scatter(
        terms.astype(jnp.bfloat16), "mp", scatter_dimension=0, tiled=True
    ).astype(jnp.float32)
    layer_output = layer_input + attn_out + branch_sum + full_down_bias.astype(jnp.float32)[None, :]
    grad_low = cotangent.astype(jnp.bfloat16)
    bias_grad = jnp.sum(cotangent, axis=0)
    grad_rows = lax.all_gather(grad_low, "mp", axis=0, tiled=True)
    head_grads = (
        jnp.dot(grad_rows, dense_local, preferred_element_type=jnp.float32)
        .astype(jnp.bfloat16)
        .reshape(group_rows, local_heads, head_dim)
    )
    row_delta = jnp.sum(head_grads.astype(jnp.float32) * out_heads.astype(jnp.float32), axis=-1).T

    def block_grads(pair, key_segs, causal):
        scores, key_mask = block_scores(pair, key_segs, causal)
        attn_probs = jnp.where(key_mask, jnp.exp(scores - row_lse[..., None]), 0.0)
        key_block = pair[:, 0].reshape(group_rows, local_heads, head_dim)
        value_block = pair[:, 1].reshape(group_rows, local_heads, head_dim)
        prob_grads = jnp.einsum(
            "qhd,khd->hqk", head_grads, value_block, preferred_element_type=jnp.float32
        )
        score_grads = (attn_probs * (prob_grads - row_delta[..., None]) * score_scale).astype(
            jnp.bfloat16
        )
        query_grads = jnp.einsum(
            "hqk,khd->qhd", score_grads, key_block, preferred_element_type=jnp.float32
        )
        key_part = jnp.einsum(
            "hqk,qhd->khd", score_grads, query_rows, preferred_element_type=jnp.float32
        )
        value_part = jnp.einsum(
            "hqk,qhd->khd",
            attn_probs.astype(jnp.bfloat16),
            head_grads,
            preferred_element_type=jnp.float32,
        )
        return (
            query_grads,
            jnp.stack(
                [
                    key_part.reshape(group_rows, local_width),
                    value_part.reshape(group_rows, local_width),
                ],
                axis=1,
            ),
        )

    zero_pair = jnp.zeros((group_rows, 2, local_width), jnp.float32)
    query_grads, pair_grads = block_grads(own_pair, group_seg, True)
    for pair, key_segs, distance in key_sets:
        query_part, sent_back = lax.cond(
            is_live(key_segs),
            lambda: block_grads(pair, key_segs, False),
            lambda: (zero_heads, zero_pair),
        )
        query_grads = query_grads + query_part
        pair_grads = pair_grads + from_behind(sent_back, "fsdp", -distance)
    key_grads = rotate_back(
        pair_grads[:, 0].reshape(group_rows, local_heads, head_dim), group_cos, group_sin
    )
    query_back = rotate_back(query_grads, group_cos, group_sin)
    head_stack = jnp.stack(
        [
            query_back.reshape(group_rows, local_width),
            key_grads.reshape(group_rows, local_width),
            pair_grads[:, 1],
        ],
        axis=1,
    ).astype(jnp.bfloat16)
    qkv_grads = lax.all_to_all(head_stack, "mp", split_axis=0, concat_axis=2, tiled=True).reshape(
        tok_dev, 3 * model_width
    )
    qkv_w_part = contract_rows(h_attn, qkv_grads).reshape(model_width, 3, head_count, head_dim)
    dense_part = contract_rows(grad_low, attn_heads).reshape(model_width, 1, head_count, head_dim)
    heavy_grads = jnp.concatenate([qkv_w_part, dense_part], axis=1)
    grad_qkv_b = jnp.sum(qkv_grads.astype(jnp.float32), axis=0)
    attn_input_grad = contract_cols(qkv_grads, w_qkv)
    hidden_grads = jnp.dot(grad_rows, full_down, preferred_element_type=jnp.float32) * gelu_slope(
        pre_act
    )
    hidden_low = hidden_grads.astype(jnp.bfloat16)
    grad_down_w = contract_rows(grad_rows, activation)
    grad_up_w = contract_rows(mlp_rows, hidden_low)
    grad_up_b = lax.dynamic_update_slice_in_dim(
        jnp.zeros((full_up_bias.shape[0],), jnp.float32),
        jnp.sum(hidden_grads, axis=0),
        model_rank * hidden_local,
        0,
    )
    row_part = hidden_low
    terms = contract_cols(row_part, full_up)
    input_sums = lax.psum_scatter(terms, "mp", scatter_dimension=0, tiled=True)
    grad_gain_attn = jnp.sum(attn_input_grad * normed, axis=0)
    grad_beta_attn = jnp.sum(attn_input_grad, axis=0)
    grad_gain_mlp = jnp.sum(input_sums * normed, axis=0)
    grad_beta_mlp = jnp.sum(input_sums, axis=0)
    grad_hat = attn_input_grad * gain_one + input_sums * gain_two
    input_grad = cotangent + norm_back(grad_hat, normed, inv_std)
    reduced = (
        lax.psum_scatter(grad_qkv_b, "fsdp", scatter_dimension=0, tiled=True),
        lax.psum_scatter(bias_grad, "fsdp", scatter_dimension=0, tiled=True),
        lax.psum_scatter(grad_up_b, "fsdp", scatter_dimension=0, tiled=True),
        lax.psum_scatter(grad_gain_attn, "fsdp", scatter_dimension=0, tiled=True),
        lax.psum_scatter(grad_beta_attn, "fsdp", scatter_dimension=0, tiled=True),
        lax.psum_scatter(grad_gain_mlp, "fsdp", scatter_dimension=0, tiled=True),
        lax.psum_scatter(grad_beta_mlp, "fsdp", scatter_dimension=0, tiled=True),
        lax.psum_scatter(heavy_grads, "fsdp", scatter_dimension=0, tiled=True),
        lax.psum_scatter(grad_up_w, "fsdp", scatter_dimension=0, tiled=True),
        lax.psum_scatter(grad_down_w, "fsdp", scatter_dimension=0, tiled=True),
    )
    heavy_owned = reduced[7]
    joined = lax.psum(
        (
            reduced[0],
            reduced[1],
            reduced[2],
            reduced[3],
            reduced[4],
            reduced[5],
            reduced[6],
            heavy_owned,
        ),
        "mp",
    )
    heavy_sum = joined[7]
    grad_qkv_w = heavy_sum[:, :3]
    grad_dense_w = heavy_sum[:, 3].reshape(heavy_sum.shape[0], model_width).T
    return (
        layer_output,
        input_grad,
        grad_qkv_w,
        joined[0],
        grad_dense_w,
        joined[1],
        joined[3],
        joined[4],
        joined[5],
        joined[6],
        reduced[8],
        joined[2],
        reduced[9],
        joined[1],
    )


def solution(mesh):
    placed = (
        P(("fsdp", "mp"), None),
        P(("fsdp", "mp"), None),
        P(),
        P("fsdp"),
        P("fsdp"),
        P("fsdp"),
        P("fsdp"),
        P("fsdp", None, None, None),
        P("fsdp"),
        P(None, "fsdp"),
        P("fsdp"),
        P("fsdp", "mp"),
        P("fsdp"),
        P("fsdp", "mp"),
        P("fsdp"),
    )
    return jax.shard_map(
        on_device,
        mesh=mesh,
        in_specs=placed,
        out_specs=(
            P(("fsdp", "mp"), None),
            P(("fsdp", "mp"), None),
            P("fsdp", None, None, None),
            P("fsdp"),
            P(None, "fsdp"),
            P("fsdp"),
            P("fsdp"),
            P("fsdp"),
            P("fsdp"),
            P("fsdp"),
            P("fsdp", "mp"),
            P("fsdp"),
            P("fsdp", "mp"),
            P("fsdp"),
        ),
        check_vma=False,
    )
```

profile of v0, /device:TPU:0, one launch (start us, length us, event | category | flops | bytes accessed | tf_op | source)
XLA Modules:
  0.0 617.0 jit_solution(12279825027191163259)
XLA Ops:
  7.3 2.5 copy.159
  16.6 27.1 %all-reduce.16 = (bf16[2304]{0:T(1024)(128)(2,1)S(1)}, bf16[768]{0:T(1024)(128)(2,1)S(1)}, bf16[768]{0:T(1024)(128)(2,1)S(1)}, bf16[768]{0:T(1024)(128)(2,1)}, b...) all-reduce(bf16[2304]{0:T(1024)(128)(2,1)S(1)} %dynamic-update-slic, ...), channel_id=1, replica_groups=mesh['fsdp'=8,'mp'=4] {'fsdp'}, use_global_device_ids=true, to_apply=%add.2 | all-reduce | flops 6912 | bytes 27648
  43.8 28.4 %all-gather.6.cloned.1.call-done = bf16[768,3,12,64]{3,2,1,0:T(8,128)(2,1)} async-done(((bf16[96,3,12,64]{3,2,1,0:T(8,128)(2,1)}), bf16[768,3,12,64]{3,2,1,0:T(8,128)(2,1)}) %all-gather.6.cloned.1.call-update) | async-done | bytes 3538960 | tf_op jit(solution)/shard_map/all_gather | solution.py:150
  72.2 10.8 %copy.160 = bf16[768,3,12,64]{0,3,2,1:T(8,128)(2,1)} copy(bf16[768,3,12,64]{3,2,1,0:T(8,128)(2,1)} %all-gather.6.cloned.1.call-done) | data formatting | bytes 7077888 | tf_op jit(solution)/shard_map/all_gather | solution.py:150
  83.1 3.3 convolution_add_fusion
  88.5 4.6 all-to-all-start
  94.7 18.9 %all-to-all-done = bf16[128,3,768]{0,1,2:T(4,128)(2,1)S(1)} async-done(((bf16[128,3,768]{0,1,2:T(4,128)(2,1)}), bf16[128,3,768]{0,1,2:T(4,128)(2,1)S(1)}, u32[]{:S(2)}, u32[]{:S(2)}) %all-to-all-start) | async-done | bytes 589856 | tf_op jit(solution)/shard_map/all_to_all | solution.py:200
  116.5 10.0 %collective-permute-start.1 = (bf16[512,2,192]{0,2,1:T(8,128)(2,1)S(1)}, bf16[512,2,192]{0,2,1:T(8,128)(2,1)S(1)}, u32[]{:S(2)}, u32[]{:S(2)}) collective-permute-start(bf16[512,2,192]{0,2,1:T(8,128)(2,1)S(1)} %collective-permute-done), channel_id=1, source_target_pairs={{0,4},{4,8},{8,12},{12,16},{16,20},{20,24},{24,28},{1,5},{5,9},{9,... | collective-permute-start | bytes 1179656 | tf_op jit(solution)/shard_map/ppermute | solution.py:19
  134.6 17.9 %all_gather.55 = bf16[512,768]{1,0:T(8,128)(2,1)S(1)} all-gather(bf16[128,768]{1,0:T(8,128)(2,1)S(1)} %get-tuple-element.530), channel_id=1, replica_groups=mesh['fsdp'=8,'mp'=4] {'mp'}, dimensions={0}, use_global_device_ids=true | all-gather | bytes 983040 | tf_op jit(solution)/shard_map/all_gather | solution.py:284
  152.5 2.3 collective-permute-start.2
  154.8 2.4 convolution_convert_fusion.1
  157.9 5.5 collective-permute-start.3
  163.5 1.7 select_reduce_fusion.5
  166.8 1.8 select_reduce_fusion.4
  170.3 3.4 convolution_bitcast_fusion.6
  174.5 2.0 conditional.19
  176.5 2.0 multiply_reduce_fusion.3
  178.5 3.4 multiply_convert_fusion.4
  184.7 3.6 all-to-all-start.1
  200.1 17.8 %collective-permute-done.7 = f32[512,2,192]{0,2,1:T(8,128)} collective-permute-done((f32[512,2,192]{0,2,1:T(8,128)}, f32[512,2,192]{0,2,1:T(8,128)}, u32[]{:S(2)}, u32[]{:S(2)}) %collective-permute-start.7) | collective-permute-done | bytes 786464 | tf_op jit(solution)/shard_map/ppermute | solution.py:19
  218.0 5.6 collective-permute-done.6
  223.5 2.1 fusion.56
  227.3 4.8 all-to-all-start.2
  232.5 15.6 %all-to-all-done.2 = bf16[512,3,192]{2,1,0:T(4,128)(2,1)} async-done(((bf16[512,3,192]{2,1,0:T(4,128)(2,1)}), bf16[512,3,192]{2,1,0:T(4,128)(2,1)}, u32[]{:S(2)}, u32[]{:S(2)}) %all-to-all-start.2) | async-done | bytes 589856 | tf_op jit(solution)/shard_map/all_to_all | solution.py:348
  251.0 4.6 pad_maximum_fusion.4
  255.6 9.6 %copy.189 = f32[768,3072]{1,0:T(8,128)} copy(f32[768,3072]{0,1:T(8,128)} %bitcast.239) | data formatting | bytes 18874368
  265.9 52.3 %all-gather = bf16[8,1,384]{2,1,0:T(2,128)(2,1)S(1)} all-gather(bf16[1,1,384]{2,1,0:T(2,128)(2,1)S(1)} %reshape.696), channel_id=1, replica_groups=mesh['fsdp'=8,'mp'=4] {'fsdp'}, dimensions={0}, use_global_device_ids=true | all-gather | bytes 6912 | tf_op jit(solution)/shard_map/all_gather | solution.py:156
  318.5 17.9 %all_gather.50 = bf16[512,768]{1,0:T(8,128)(2,1)S(1)} all-gather(bf16[128,768]{1,0:T(8,128)(2,1)S(1)} %add_convert_fusion), channel_id=1, replica_groups=mesh['fsdp'=8,'mp'=4] {'mp'}, dimensions={0}, use_global_device_ids=true | all-gather | bytes 983040 | tf_op jit(solution)/shard_map/all_gather | solution.py:201
  336.4 3.3 multiply_convert_fusion.5
  339.7 3.4 convolution_convert_fusion
  343.2 3.6 fusion.83
  347.7 2.0 fusion.59
  349.8 34.0 %reduce-scatter.16.cloned.1.call-done = f32[96,3072]{1,0:T(8,128)} async-done(((f32[768,3072]{1,0:T(8,128)}), f32[96,3072]{1,0:T(8,128)}) %reduce-scatter.16.cloned.1.call-update) | async-done | bytes 1179664
  383.7 2.9 copy.190
  387.0 2.3 fusion.57
  389.3 2.2 convolution_bitcast_fusion.4
  391.5 2.0 copy.187
  397.7 12.0 %reduce-scatter.10.cloned.1.call-done = bf16[128,768]{1,0:T(8,128)(2,1)} async-done(((bf16[512,768]{1,0:T(8,128)(2,1)}), bf16[128,768]{1,0:T(8,128)(2,1)}) %reduce-scatter.10.cloned.1.call-update) | async-done | bytes 196624 | tf_op jit(solution)/shard_map/reduce_scatter | solution.py:278
  409.7 2.6 fusion.52
  412.3 2.2 copy.183
  415.4 31.6 %reduce-scatter.12.cloned.1.call-done = f32[128,768]{1,0:T(8,128)} async-done(((f32[512,768]{1,0:T(8,128)}), f32[128,768]{1,0:T(8,128)}) %reduce-scatter.12.cloned.1.call-update) | async-done | bytes 393232 | tf_op jit(solution)/shard_map/reduce_scatter | solution.py:370
  446.9 2.9 multiply_reduce_fusion
  449.9 25.2 %all-reduce.14 = (f32[2304]{0:T(1024)S(1)}, f32[768]{0:T(1024)S(1)}, f32[768]{0:T(1024)S(1)}, f32[768]{0:T(1024)S(1)}, f32[768]{0:T(1024)S(1)}, /*index=5*/f32[768]{0:T(1024)S(1)}, f32[3072]{0:T(1024)S(1)}) all-reduce(f32[2304]{0:T(1024)S(1)} %reduce_sum.242, ...), channel_id=5, replica_groups=mesh['fsdp'=8,'mp'=4] {'fsdp'}, use_global_device_ids=true, to_apply=%region_53.54.clone | all-reduce | flops 9216 | bytes 73728
  475.7 10.4 %all-reduce.15 = (f32[288]{0:T(512)}, f32[96]{0:T(128)S(1)}, f32[96]{0:T(128)}, f32[96]{0:T(128)}, f32[96]{0:T(128)}, /*index=5*/f32[96]{0:T(128)}, f32[384]{0:T(512)}) all-reduce(f32[288]{0:T(512)S(1)} %dynamic-slice.8, f32[96]{0:T(128)S(1)} %dynamic-slice.10, f32[96]{0:T(128)S(1)} %dynamic-slice.12, ...), channel_id=1, replica_groups=mesh['fsdp'=8,'mp'=4] {'mp'}, use_global_device_ids=true, to_apply=%region_54.55 | all-reduce | flops 1152 | bytes 9216 | tf_op jit(solution)/shard_map/psum | solution.py:390
  487.0 30.6 %all-reduce.19.cloned.1.call-done = f32[96,4,12,64]{0,3,2,1:T(8,128)} async-done(((f32[96,4,12,64]{0,3,2,1:T(8,128)}), f32[96,4,12,64]{0,3,2,1:T(8,128)}) %all-reduce.19.cloned.1.call-update) | async-done | bytes 1179664 | tf_op jit(solution)/shard_map/psum | solution.py:390
  519.5 2.4 slice.228
  521.9 41.2 %reduce-scatter.14.cloned.1.call-done = f32[96,768]{1,0:T(8,128)} async-done(((f32[768,768]{1,0:T(8,128)}), f32[96,768]{1,0:T(8,128)}) %reduce-scatter.14.cloned.1.call-update) | async-done | bytes 294928 | tf_op jit(solution)/shard_map/reduce_scatter | solution.py:386
  563.1 46.1 %reduce-scatter.18.cloned.1.call-done = f32[96,768]{1,0:T(8,128)} async-done(((f32[768,768]{1,0:T(8,128)}), f32[96,768]{1,0:T(8,128)}) %reduce-scatter.18.cloned.1.call-update) | async-done | bytes 294928
  (273 shorter events, 51.6 us)
Async XLA Ops:
  7.2 7.7 %copy-start.60 = (bf16[96]{0:T(256)(128)(2,1)S(1)}, bf16[96]{0:T(256)(128)(2,1)}, u32[]{:S(2)}) copy-start(bf16[96]{0:T(256)(128)(2,1)} %param.53) | copy-start | bytes 580
  7.2 7.9 %copy-start.61 = (bf16[96]{0:T(256)(128)(2,1)S(1)}, bf16[96]{0:T(256)(128)(2,1)}, u32[]{:S(2)}) copy-start(bf16[96]{0:T(256)(128)(2,1)} %param.44) | copy-start | bytes 580
  7.2 8.1 %copy-start.62 = (bf16[96]{0:T(256)(128)(2,1)S(1)}, bf16[96]{0:T(256)(128)(2,1)}, u32[]{:S(2)}) copy-start(bf16[96]{0:T(256)(128)(2,1)} %param.45) | copy-start | bytes 580
  7.2 8.3 %copy-start.63 = (bf16[96]{0:T(256)(128)(2,1)S(1)}, bf16[96]{0:T(256)(128)(2,1)}, u32[]{:S(2)}) copy-start(bf16[96]{0:T(256)(128)(2,1)} %param.42) | copy-start | bytes 580
  7.3 8.6 %copy-start.64 = (bf16[96]{0:T(256)(128)(2,1)S(1)}, bf16[96]{0:T(256)(128)(2,1)}, u32[]{:S(2)}) copy-start(bf16[96]{0:T(256)(128)(2,1)} %param.43) | copy-start | bytes 580
  7.3 8.8 %copy-start.65 = (bf16[96]{0:T(256)(128)(2,1)S(1)}, bf16[96]{0:T(256)(128)(2,1)}, u32[]{:S(2)}) copy-start(bf16[96]{0:T(256)(128)(2,1)} %param.49) | copy-start | bytes 580
  7.3 9.0 %copy-start.56 = (bf16[288]{0:T(512)(128)(2,1)S(1)}, bf16[288]{0:T(512)(128)(2,1)}, u32[]{:S(2)}) copy-start(bf16[288]{0:T(512)(128)(2,1)} %param.47) | copy-start | bytes 1732
  7.3 64.9 %all-gather.6.cloned.1.call-start = ((), (), s32[]{:S(2)}) async-start(), calls=%async_computation.8 | async-start | bytes 10616832 | tf_op jit(solution)/shard_map/all_gather | solution.py:150
  9.9 144.9 %all-gather.8.cloned.1.call-start = ((), (), s32[]{:S(2)}) async-start(), calls=%async_computation.9 | async-start | bytes 1327104 | tf_op jit(solution)/shard_map/all_gather | solution.py:151
  10.6 325.8 %all-gather.10.cloned.1.call-start = ((), (), s32[]{:S(2)}) async-start(), calls=%async_computation.10 | async-start | bytes 1327104 | tf_op jit(solution)/shard_map/all_gather | solution.py:152
  11.4 328.3 %all-gather.12.cloned.1.call-start = ((), (), s32[]{:S(2)}) async-start(), calls=%async_computation.11 | async-start | bytes 1327104 | tf_op jit(solution)/shard_map/all_gather | solution.py:153
  14.3 68.8 %copy-start.34 = (f32[128]{0:T(128)}, f32[128]{0:T(128)S(1)}, u32[]{:S(2)}) copy-start(f32[128]{0:T(128)S(1)} %broadcast_multiply_fusion.2) | copy-start | bytes 1540
  14.5 68.6 %copy-start.37 = (f32[128]{0:T(128)}, f32[128]{0:T(128)S(1)}, u32[]{:S(2)}) copy-start(f32[128]{0:T(128)S(1)} %add_rsqrt_fusion) | copy-start | bytes 1540
  87.1 28.1 %copy-start.18 = (f32[128,768]{1,0:T(8,128)S(1)}, f32[128,768]{1,0:T(8,128)}, u32[]{:S(2)}) copy-start(f32[128,768]{1,0:T(8,128)} %param.40) | copy-start | bytes 1179652
  88.5 25.1 %all-to-all-start = ((bf16[128,3,768]{0,1,2:T(4,128)(2,1)}), bf16[128,3,768]{0,1,2:T(4,128)(2,1)S(1)}, u32[]{:S(2)}, u32[]{:S(2)}) async-start(bf16[128,3,768]{0,1,2:T(4,128)(2,1)} %copy.162), calls=%async_computation | async-start | bytes 1572864 | tf_op jit(solution)/shard_map/all_to_all | solution.py:200
  93.1 76.0 %copy-start.32 = (s32[512]{0:T(512)}, s32[512]{0:T(512)S(1)}, u32[]{:S(2)}) copy-start(s32[512]{0:T(512)S(1)} %compare_select_fusion.2) | copy-start | bytes 6148
  113.8 2.6 collective-permute-start
  115.2 53.4 %copy-start.30 = (s32[512]{0:T(512)}, s32[512]{0:T(512)S(1)}, u32[]{:S(2)}) copy-start(s32[512]{0:T(512)S(1)} %compare_select_fusion.1) | copy-start | bytes 6148
  115.8 38.9 %copy-start.11 = (bf16[128,768]{1,0:T(8,128)(2,1)}, bf16[128,768]{1,0:T(8,128)(2,1)S(1)}, u32[]{:S(2)}) copy-start(bf16[128,768]{1,0:T(8,128)(2,1)S(1)} %get-tuple-element.530) | copy-start | bytes 589828
  116.5 36.0 %collective-permute-start.1 = (bf16[512,2,192]{0,2,1:T(8,128)(2,1)S(1)}, bf16[512,2,192]{0,2,1:T(8,128)(2,1)S(1)}, u32[]{:S(2)}, u32[]{:S(2)}) collective-permute-start(bf16[512,2,192]{0,2,1:T(8,128)(2,1)S(1)} %collective-permute-done), channel_id=1, source_target_pairs={{0,4},{4,8},{8,12},{12,16},{16,20},{20,24},{24,28},{1,5},{5,9},{9,... | collective-permute-start | bytes 1179656 | tf_op jit(solution)/shard_map/ppermute | solution.py:19
  126.5 42.6 %copy-start.33 = (s32[512]{0:T(512)}, s32[512]{0:T(512)S(1)}, u32[]{:S(2)}) copy-start(s32[512]{0:T(512)S(1)} %compare_select_fusion.3) | copy-start | bytes 6148
  152.5 12.7 %copy-start.3 = (bf16[512,768]{1,0:T(8,128)(2,1)}, bf16[512,768]{1,0:T(8,128)(2,1)S(1)}, u32[]{:S(2)}) copy-start(bf16[512,768]{1,0:T(8,128)(2,1)S(1)} %all_gather.55) | copy-start | bytes 2359300
  152.5 5.4 collective-permute-start.2
  157.9 11.2 %collective-permute-start.3 = (bf16[512,2,192]{0,2,1:T(8,128)(2,1)S(1)}, bf16[512,2,192]{0,2,1:T(8,128)(2,1)S(1)}, u32[]{:S(2)}, u32[]{:S(2)}) collective-permute-start(bf16[512,2,192]{0,2,1:T(8,128)(2,1)S(1)} %collective-permute-done.2), channel_id=1, source_target_pairs={{0,4},{4,8},{8,12},{12,16},{16,20},{20,24},{24,28},{1,5},{5,9},{9,... | collective-permute-start | bytes 1179656 | tf_op jit(solution)/shard_map/ppermute | solution.py:19
  184.7 42.6 %all-to-all-start.1 = ((bf16[4,128,192]{1,2,0:T(8,128)(2,1)}), bf16[4,128,192]{1,2,0:T(8,128)(2,1)S(1)}, u32[]{:S(2)}, u32[]{:S(2)}) async-start(bf16[4,128,192]{1,2,0:T(8,128)(2,1)} %copy.166), calls=%async_computation.1 | async-start | bytes 393216 | tf_op jit(solution)/shard_map/all_to_all | solution.py:268
  189.3 28.6 %collective-permute-start.7 = (f32[512,2,192]{0,2,1:T(8,128)}, f32[512,2,192]{0,2,1:T(8,128)}, u32[]{:S(2)}, u32[]{:S(2)}) collective-permute-start(f32[512,2,192]{0,2,1:T(8,128)} %get-tuple-element.299), channel_id=1, source_target_pairs={{16,0},{20,4},{24,8},{28,12},{17,1},{21,5},{25,9},{29,13},{18,2},{... | collective-permute-start | bytes 2359304 | tf_op jit(solution)/shard_map/ppermute | solution.py:19
  191.7 31.9 %collective-permute-start.6 = (f32[512,2,192]{0,2,1:T(8,128)}, f32[512,2,192]{0,2,1:T(8,128)}, u32[]{:S(2)}, u32[]{:S(2)}) collective-permute-start(f32[512,2,192]{0,2,1:T(8,128)} %get-tuple-element.298), channel_id=1, source_target_pairs={{12,0},{16,4},{20,8},{24,12},{28,16},{13,1},{17,5},{21,9},{25,13},... | collective-permute-start | bytes 2359304 | tf_op jit(solution)/shard_map/ppermute | solution.py:19
  194.0 29.5 %collective-permute-start.5 = (f32[512,2,192]{0,2,1:T(8,128)}, f32[512,2,192]{0,2,1:T(8,128)}, u32[]{:S(2)}, u32[]{:S(2)}) collective-permute-start(f32[512,2,192]{0,2,1:T(8,128)} %get-tuple-element.297), channel_id=1, source_target_pairs={{8,0},{12,4},{16,8},{20,12},{24,16},{28,20},{9,1},{13,5},{17,9},{2... | collective-permute-start | bytes 2359304 | tf_op jit(solution)/shard_map/ppermute | solution.py:19
  195.8 27.8 %collective-permute-start.4 = (f32[512,2,192]{0,2,1:T(8,128)S(1)}, f32[512,2,192]{0,2,1:T(8,128)S(1)}, u32[]{:S(2)}, u32[]{:S(2)}) collective-permute-start(f32[512,2,192]{0,2,1:T(8,128)S(1)} %get-tuple-element.296), channel_id=1, source_target_pairs={{4,0},{8,4},{12,8},{16,12},{20,16},{24,20},{28,24},{5,1},{9,5},{13... | collective-permute-start | bytes 2359304 | tf_op jit(solution)/shard_map/ppermute | solution.py:19
  200.1 25.5 %copy-start.28 = (f32[512,8]{0,1:T(8,128)S(1)}, f32[512,8]{0,1:T(8,128)}, u32[]{:S(2)}) copy-start(f32[512,8]{0,1:T(8,128)} %get-tuple-element.535) | copy-start | bytes 49156
  200.1 25.5 %copy-start.29 = (f32[512,8]{0,1:T(8,128)S(1)}, f32[512,8]{0,1:T(8,128)}, u32[]{:S(2)}) copy-start(f32[512,8]{0,1:T(8,128)} %get-tuple-element.536) | copy-start | bytes 49156
  227.3 22.5 %copy-start.35 = (f32[128]{0:T(128)S(1)}, f32[128]{0:T(128)}, u32[]{:S(2)}) copy-start(f32[128]{0:T(128)} %copy-done.34) | copy-start | bytes 1540
  227.3 22.5 %copy-start.38 = (f32[128]{0:T(128)S(1)}, f32[128]{0:T(128)}, u32[]{:S(2)}) copy-start(f32[128]{0:T(128)} %copy-done.37) | copy-start | bytes 1540
  227.3 20.9 %copy-start.9 = (bf16[4,128,192]{1,2,0:T(8,128)(2,1)}, bf16[4,128,192]{1,2,0:T(8,128)(2,1)S(1)}, u32[]{:S(2)}) copy-start(bf16[4,128,192]{1,2,0:T(8,128)(2,1)S(1)} %all-to-all-done.1) | copy-start | bytes 589828
  227.3 20.9 %all-to-all-start.2 = ((bf16[512,3,192]{2,1,0:T(4,128)(2,1)}), bf16[512,3,192]{2,1,0:T(4,128)(2,1)}, u32[]{:S(2)}, u32[]{:S(2)}) async-start(bf16[512,3,192]{2,1,0:T(4,128)(2,1)} %copy.171), calls=%async_computation.3 | async-start | bytes 2097152 | tf_op jit(solution)/shard_map/all_to_all | solution.py:348
  232.1 151.6 %reduce-scatter.16.cloned.1.call-start = ((), (), s32[]{:S(2)}) async-start(), calls=%async_computation.16 | async-start | bytes 10616832
  265.2 53.1 %copy-start.39 = (f32[128]{0:T(128)S(1)}, f32[128]{0:T(128)}, u32[]{:S(2)}) copy-start(f32[128]{0:T(128)} %copy-done.37) | copy-start | bytes 1540
  265.2 144.4 %reduce-scatter.10.cloned.1.call-start = ((), (), s32[]{:S(2)}) async-start(), calls=%async_computation.12 | async-start | bytes 983040 | tf_op jit(solution)/shard_map/reduce_scatter | solution.py:278
  343.1 103.8 %reduce-scatter.12.cloned.1.call-start = ((), (), s32[]{:S(2)}) async-start(), calls=%async_computation.13 | async-start | bytes 1966080 | tf_op jit(solution)/shard_map/reduce_scatter | solution.py:370
  349.7 37.3 %copy-start.26 = (bf16[512,768]{1,0:T(8,128)(2,1)S(1)}, bf16[512,768]{1,0:T(8,128)(2,1)}, u32[]{:S(2)}) copy-start(bf16[512,768]{1,0:T(8,128)(2,1)} %copy-done.25) | copy-start | bytes 2359300
  349.7 167.9 %all-reduce.19.cloned.1.call-start = ((), (), s32[]{:S(2)}) async-start(), calls=%async_computation.14 | async-start | bytes 3145728 | tf_op jit(solution)/shard_map/psum | solution.py:390
  386.7 176.4 %reduce-scatter.14.cloned.1.call-start = ((), (), s32[]{:S(2)}) async-start(), calls=%async_computation.15 | async-start | bytes 2654208 | tf_op jit(solution)/shard_map/reduce_scatter | solution.py:386
  389.3 219.9 %reduce-scatter.18.cloned.1.call-start = ((), (), s32[]{:S(2)}) async-start(), calls=%async_computation.17 | async-start | bytes 2654208
  391.5 18.2 %copy-start.10 = (bf16[4,128,192]{1,2,0:T(8,128)(2,1)S(1)}, bf16[4,128,192]{1,2,0:T(8,128)(2,1)}, u32[]{:S(2)}) copy-start(bf16[4,128,192]{1,2,0:T(8,128)(2,1)} %copy-done.9) | copy-start | bytes 589828
  393.5 53.4 %copy-start.40 = (f32[128]{0:T(128)S(1)}, f32[128]{0:T(128)}, u32[]{:S(2)}) copy-start(f32[128]{0:T(128)} %copy-done.37) | copy-start | bytes 1540
  414.4 35.4 %copy-start.36 = (f32[768]{0:T(1024)S(1)}, f32[768]{0:T(1024)}, u32[]{:S(2)}) copy-start(f32[768]{0:T(1024)} %get-tuple-element.529) | copy-start | bytes 9220
  414.5 71.6 %copy-start.19 = (f32[128,768]{1,0:T(8,128)S(1)}, f32[128,768]{1,0:T(8,128)}, u32[]{:S(2)}) copy-start(f32[128,768]{1,0:T(8,128)} %param.40) | copy-start | bytes 1179652
  486.1 123.7 %copy-start.66 = (f32[96]{0:T(128)}, f32[96]{0:T(128)S(1)}, u32[]{:S(2)}) copy-start(f32[96]{0:T(128)S(1)} %get-tuple-element.614) | copy-start | bytes 1156
  (27 other events, 83.7 us)
Sparse Core Ops, SparseCore 0:
  10.5 61.6 all-gather.5
  74.1 23.9 all-gather.7
  99.9 25.5 all-gather.9
  127.3 23.9 all-gather.11
  265.4 118.3 reduce-scatter.15
  386.5 23.1 reduce-scatter.9
  412.0 34.9 reduce-scatter.11
  449.3 68.2 all-reduce.18
  521.5 41.5 reduce-scatter.13
  566.8 42.3 reduce-scatter.17
where the time goes:
time: 627 us; the launch traced here: 617 us
  waiting for transfers between devices  284 us (45%)
  blocking collectives  151 us (24%)
  local copies, waits for them, and re-layouts  57.7 us (9%)
  matrix products  40.5 us (6%)
  starting transfers between devices  38.1 us (6%)
  between operations  24.1 us (4%)
  other arithmetic  18.6 us (3%)
    unnamed x12, waiting for transfers between devices  82.1 us
    unnamed x2, blocking collectives  52.4 us
    all_gather x1, blocking collectives, on_device(): lax.all_gather(up_bias, 'fsdp', axis=0, tiled=True)  52.3 us
    reduce_scatter x1, waiting for transfers between devices, on_device(): lax.psum_scatter(grad_up_w, 'fsdp', scatter_dimension=0, tiled=True)  41.2 us
    reduce_scatter x1, waiting for transfers between devices, on_device(): input_sums = lax.psum_scatter(terms, 'mp', scatter_dimension=0, tiled=True)  31.6 us
    psum x1, waiting for transfers between devices, on_device(): lax.psum((reduced[0], reduced[1], reduced[2], reduced[3], reduced[4], red...  30.6 us
    all_gather x1, waiting for transfers between devices, on_device(): lax.all_gather(qkv_weight, 'fsdp', axis=0, tiled=True)  28.4 us
    unnamed x137, local copies, waits for them, and re-layouts  25.5 us
  transfers between devices with their start and end apart: 21, of which 12 were waited for; matrix products, arithmetic and copies ran while one was open for 17% of the time, Pallas kernels for 0%

commit v1 on v0

v1 whole, which is shorter than its diff:
```python
import functools
import math

import jax
import jax.numpy as jnp
from jax import lax
from jax.experimental import pallas as pl
from jax.experimental.pallas import tpu as pltpu
from jax.sharding import PartitionSpec as P

ROT = 16
SPAN = 16


EPS = 1e-05
NEG_FILL = -1e30


def norm_parts(inputs):
    row_mean = jnp.mean(inputs, axis=-1, keepdims=True)
    centred = inputs - row_mean
    row_var = jnp.mean(centred * centred, axis=-1, keepdims=True)
    inv_std = lax.rsqrt(row_var + EPS)
    return (centred * inv_std, inv_std)


def norm_back(grad_hat, normed, inv_std):
    first_mean = jnp.mean(grad_hat, axis=-1, keepdims=True)
    second_mean = jnp.mean(grad_hat * normed, axis=-1, keepdims=True)
    return inv_std * (grad_hat - first_mean - normed * second_mean)


def gelu_value(pre_act):
    return 0.5 * pre_act * (1.0 + lax.erf(pre_act * (1.0 / math.sqrt(2.0))))


def gelu_slope(pre_act):
    cumulative = 0.5 * (1.0 + lax.erf(pre_act * (1.0 / math.sqrt(2.0))))
    return cumulative + pre_act * jnp.exp(-0.5 * pre_act * pre_act) * (
        1.0 / math.sqrt(2.0 * math.pi)
    )


def rotary_tables(positions):
    half_rot = ROT // 2
    inverse = jnp.exp(jnp.arange(half_rot, dtype=jnp.float32) * (-2.0 * math.log(10000.0) / ROT))
    phase_angle = positions.astype(jnp.float32)[:, None] * inverse[None, :]
    return (jnp.cos(phase_angle)[:, None, :], jnp.sin(phase_angle)[:, None, :])


def rotate(vectors, cosine, sine_table):
    half_rot = ROT // 2
    first_half = vectors[..., :half_rot]
    second_half = vectors[..., half_rot:ROT]
    return jnp.concatenate(
        [
            first_half * cosine - second_half * sine_table,
            second_half * cosine + first_half * sine_table,
            vectors[..., ROT:],
        ],
        axis=-1,
    )


def rotate_back(grads, cosine, sine_table):
    half_rot = ROT // 2
    first_half = grads[..., :half_rot]
    second_half = grads[..., half_rot:ROT]
    return jnp.concatenate(
        [
            first_half * cosine + second_half * sine_table,
            second_half * cosine - first_half * sine_table,
            grads[..., ROT:],
        ],
        axis=-1,
    )


def token_segments(seq_lengths, token_index):
    seq_ends = jnp.cumsum(seq_lengths, dtype=jnp.int32)
    seq_starts = seq_ends - seq_lengths
    segment_ids = jnp.sum(
        (seq_ends[None, :] <= token_index[:, None]).astype(jnp.int32), axis=1, dtype=jnp.int32
    )
    chosen = segment_ids[:, None] == jnp.arange(seq_lengths.shape[0], dtype=jnp.int32)[None, :]
    first_token = jnp.sum(jnp.where(chosen, seq_starts[None, :], 0), axis=1, dtype=jnp.int32)
    return (segment_ids, token_index - first_token)


def contract_rows(left, right):
    return lax.dot_general(
        left, right, (((0,), (0,)), ((), ())), preferred_element_type=jnp.float32
    )


def contract_cols(left, right):
    return lax.dot_general(
        left, right, (((1,), (1,)), ((), ())), preferred_element_type=jnp.float32
    )


def place():
    rank = lax.axis_index("fsdp")
    return rank // 2, rank % 2, lax.axis_index("mp")


def enter(chip_count, model_count):
    chip, core, model = place()
    barrier = pltpu.get_barrier_semaphore()
    peers = []
    if chip_count:
        peers.append((chip * 2 + (1 - core), model))
        for step in range(1, chip_count):
            peers.append((((chip + step) % chip_count) * 2 + core, model))
    for step in range(1, model_count):
        peers.append((chip * 2 + core, (model + step) % model_count))
    for peer in peers:
        pl.semaphore_signal(
            barrier, inc=1, device_id=peer, device_id_type=pl.DeviceIdType.MESH
        )
    pl.semaphore_wait(barrier, len(peers))


class Copies:
    def __init__(self, send, recv, local):
        self.send, self.recv, self.local = send, recv, local
        self.used, self.used_local = 0, 0

    def remote(self, source, target, peer):
        index = self.used
        self.used += 1
        return pltpu.make_async_remote_copy(
            src_ref=source,
            dst_ref=target,
            send_sem=self.send.at[index],
            recv_sem=self.recv.at[index],
            device_id=peer,
            device_id_type=pl.DeviceIdType.MESH,
        )

    def within(self, source, target):
        index = self.used_local
        self.used_local += 1
        return pltpu.make_async_copy(source, target, self.local.at[index])


def model_exchange(copies, source, target, model_count, gather):
    chip, core, model = place()
    started = []
    own = copies.within(source if gather else source.at[model], target.at[model])
    own.start()
    for step in range(1, model_count):
        peer = (model + step) % model_count
        copy = copies.remote(
            source if gather else source.at[peer], target.at[model], (chip * 2 + core, peer)
        )
        copy.start()
        started.append(copy)
    return [own] + started


def gather_start(copies, source, target, chip_count):
    chip, core, model = place()
    rank = chip * 2 + core
    own = copies.within(source, target.at[rank])
    own.start()
    to_pair = copies.remote(source, target.at[rank], (chip * 2 + (1 - core), model))
    to_pair.start()
    far = []
    for step in range(1, chip_count):
        peer = ((chip + step) % chip_count) * 2 + core
        copy = copies.remote(source, target.at[rank], (peer, model))
        copy.start()
        far.append(copy)
    return [own, to_pair], far


def gather_forward(copies, target, far, chip_count):
    chip, core, model = place()
    waits = []
    for step in range(1, chip_count):
        far[step - 1].wait_recv()
        slot = ((chip + chip_count - step) % chip_count) * 2 + core
        copy = copies.remote(target.at[slot], target.at[slot], (chip * 2 + (1 - core), model))
        copy.start()
        waits.append(copy)
    return waits


def open_kernel(chip_count, model_count, w_ref, v_ref, t_ref, w_out, v_out, t_out, s, r, l):
    enter(chip_count, model_count)
    copies = Copies(s, r, l)
    tokens = model_exchange(copies, t_ref, t_out, model_count, True)
    near_v, far_v = gather_start(copies, v_ref, v_out, chip_count)
    near_w, far_w = gather_start(copies, w_ref, w_out, chip_count)
    more = gather_forward(copies, v_out, far_v, chip_count)
    more += gather_forward(copies, w_out, far_w, chip_count)
    for copy in far_v + far_w:
        copy.wait_send()
    for copy in tokens + near_v + near_w + more:
        copy.wait()


def keys_kernel(chip_count, hops, x_ref, out, s, r, l):
    enter(chip_count, 1)
    copies = Copies(s, r, l)
    chip, core, model = place()
    pair = (chip * 2 + (1 - core), model)
    near = copies.remote(x_ref, out.at[0, core], pair)
    near.start()
    far, onward = [], []
    for step in range(1, hops + 1):
        target = ((chip + step) % chip_count) * 2 + core
        far.append(copies.remote(x_ref, out.at[step, core], (target, model)))
        onward.append(copies.remote(out.at[step, core], out.at[step, core], pair))

        @pl.when(chip + step < chip_count)
        def _(copy=far[-1]):
            copy.start()

    for step in range(1, hops + 1):

        @pl.when(chip >= step)
        def _(arrived=far[step - 1], copy=onward[step - 1]):
            arrived.wait_recv()
            copy.start()

    near.wait()
    for step in range(1, hops + 1):

        @pl.when(chip >= step)
        def _(copy=onward[step - 1]):
            copy.wait()

        @pl.when(chip + step < chip_count)
        def _(copy=far[step - 1]):
            copy.wait_send()


def pair_kernel(
    chip_count, model_count, hops, p_ref, b_ref, out, b_out, near_buf, sums, far_buf, s, r, l
):
    enter(chip_count, model_count)
    copies = Copies(s, r, l)
    chip, core, model = place()
    pair = (chip * 2 + (1 - core), model)
    near = [
        copies.remote(p_ref.at[1 - core, step], near_buf.at[step], pair)
        for step in range(hops + 1)
    ]
    for copy in near:
        copy.start()
    branch = model_exchange(copies, b_ref, b_out, model_count, False)
    far = []
    for step in list(range(1, hops + 1)) + [0]:
        near[step].wait_recv()
        total = p_ref[core, step].astype(jnp.float32) + near_buf[step].astype(jnp.float32)
        if step == 0:
            out[...] = total
            continue
        sums[step - 1] = total.astype(sums.dtype)
        target = ((chip + chip_count - step) % chip_count) * 2 + core
        far.append(copies.remote(sums.at[step - 1], far_buf.at[step - 1], (target, model)))

        @pl.when(chip >= step)
        def _(copy=far[-1]):
            copy.start()

    for step in range(1, hops + 1):

        @pl.when(chip + step < chip_count)
        def _(copy=far[step - 1], step=step):
            copy.wait_recv()
            out[...] += far_buf[step - 1].astype(jnp.float32)

    for step in range(1, hops + 1):

        @pl.when(chip >= step)
        def _(copy=far[step - 1]):
            copy.wait_send()

    for copy in near:
        copy.wait_send()
    for copy in branch:
        copy.wait()


def reduce_near(copies, source, near_buf, chip_count):
    chip, core, model = place()
    near = []
    for step in list(range(1, chip_count)) + [0]:
        target = (chip + step) % chip_count
        copy = copies.remote(
            source.at[target, 1 - core], near_buf.at[step], (chip * 2 + (1 - core), model)
        )
        copy.start()
        near.append(copy)
    return near


def reduce_far(copies, source, near_buf, sums, far_buf, out, near, chip_count):
    chip, core, model = place()
    far = []
    for index, step in enumerate(list(range(1, chip_count)) + [0]):
        target = (chip + step) % chip_count
        near[index].wait_recv()
        total = source[target, core].astype(jnp.float32) + near_buf[step].astype(jnp.float32)
        if step == 0:
            out[...] = total
            continue
        sums[step - 1] = total.astype(sums.dtype)
        copy = copies.remote(sums.at[step - 1], far_buf.at[step - 1], (target * 2 + core, model))
        copy.start()
        far.append(copy)
    return far


def reduce_end(out, far_buf, near, far):
    for index, copy in enumerate(far):
        copy.wait_recv()
        out[...] += far_buf[index].astype(jnp.float32)
    for copy in near + far:
        copy.wait_send()


def close_kernel(
    chip_count, model_count, g_ref, v_ref, b_ref, g_out, v_out, b_out,
    g_near, g_sums, g_far, v_near, v_sums, v_far, s, r, l,
):
    enter(chip_count, model_count)
    copies = Copies(s, r, l)
    v_started = reduce_near(copies, v_ref, v_near, chip_count)
    g_started = reduce_near(copies, g_ref, g_near, chip_count)
    branch = model_exchange(copies, b_ref, b_out, model_count, False)
    v_sent = reduce_far(copies, v_ref, v_near, v_sums, v_far, v_out, v_started, chip_count)
    g_sent = reduce_far(copies, g_ref, g_near, g_sums, g_far, g_out, g_started, chip_count)
    reduce_end(v_out, v_far, v_started, v_sent)
    reduce_end(g_out, g_far, g_started, g_sent)
    for copy in branch:
        copy.wait()


def last_kernel(model_count, g_ref, v_ref, g_out, v_out, s, r, l):
    enter(0, model_count)
    copies = Copies(s, r, l)
    started = model_exchange(copies, v_ref, v_out, model_count, True)
    started += model_exchange(copies, g_ref, g_out, model_count, True)
    for copy in started:
        copy.wait()


def call(kernel, number, operands, outs, spaces, out_spaces, scratch, remote, local):
    return pl.pallas_call(
        kernel,
        out_shape=[jax.ShapeDtypeStruct(shape, dtype) for shape, dtype in outs],
        in_specs=[pl.BlockSpec(memory_space=space) for space in spaces],
        out_specs=[pl.BlockSpec(memory_space=space) for space in out_spaces],
        scratch_shapes=scratch
        + [
            pltpu.SemaphoreType.DMA((remote,)),
            pltpu.SemaphoreType.DMA((remote,)),
            pltpu.SemaphoreType.DMA((max(local, 1),)),
        ],
        compiler_params=pltpu.CompilerParams(collective_id=number, has_side_effects=True),
    )(*operands)


def on_device(
    layer_input,
    cotangent,
    seq_lengths,
    gain_attn,
    beta_attn,
    gain_mlp,
    beta_mlp,
    qkv_weight,
    qkv_bias,
    dense_weight,
    dense_bias,
    up_weight,
    up_bias,
    down_weight,
    down_bias,
):
    fsdp_count = lax.axis_size("fsdp")
    model_count = lax.axis_size("mp")
    chip_count = fsdp_count // 2
    fsdp_rank = lax.axis_index("fsdp")
    model_rank = lax.axis_index("mp")
    chip, core = fsdp_rank // 2, fsdp_rank % 2
    tok_dev, model_width = layer_input.shape
    owned = qkv_weight.shape[0]
    head_count, head_dim = qkv_weight.shape[2:]
    local_heads = head_count // model_count
    local_width = local_heads * head_dim
    hidden_local = up_weight.shape[1]
    hidden_total = hidden_local * model_count
    group_rows = model_count * tok_dev
    key_reach = min(SPAN * group_rows, group_rows * fsdp_count // 2)
    hops = (key_reach // group_rows + 1) // 2
    score_scale = 1.0 / math.sqrt(head_dim)
    bf16, f32 = jnp.bfloat16, jnp.float32
    vmem, anywhere = pltpu.VMEM, pl.ANY

    own_qkv = lax.dynamic_slice_in_dim(qkv_weight, model_rank * local_heads, local_heads, 2)
    own_dense = lax.dynamic_slice_in_dim(dense_weight, model_rank * local_width, local_width, 0)
    pack = jnp.concatenate(
        [own_qkv.reshape(owned, 3 * local_width), own_dense.T, up_weight, down_weight], axis=1
    )
    vectors = (qkv_bias, dense_bias, up_bias, down_bias, gain_attn, beta_attn, gain_mlp, beta_mlp)
    vector_pack = jnp.concatenate(vectors).astype(f32)[None, :]
    normed, inv_std = norm_parts(layer_input)
    grad_low = cotangent.astype(bf16)
    token_pack = jnp.concatenate([normed.astype(bf16), grad_low], axis=1)
    columns = pack.shape[1]
    weights, vector_all, token_rows = call(
        functools.partial(open_kernel, chip_count, model_count),
        0,
        (pack, vector_pack, token_pack),
        [
            ((fsdp_count,) + pack.shape, bf16),
            ((fsdp_count,) + vector_pack.shape, f32),
            ((model_count,) + token_pack.shape, bf16),
        ],
        [anywhere] * 3,
        [anywhere] * 3,
        [],
        (model_count - 1) + 2 * (2 * chip_count - 1),
        3,
    )
    weights = weights.reshape(model_width, columns)
    w_qkv = weights[:, : 3 * local_width]
    w_dense = weights[:, 3 * local_width : 4 * local_width]
    w_up = weights[:, 4 * local_width : 4 * local_width + hidden_local]
    w_down = weights[:, 4 * local_width + hidden_local :]
    full = []
    at = 0
    for vector in vectors:
        full.append(vector_all[:, 0, at : at + vector.shape[0]].reshape(-1))
        at += vector.shape[0]
    full_qkv_bias, full_dense_bias, full_up_bias, full_down_bias = full[:4]
    gain_one, shift_one, gain_two, shift_two = full[4:]
    local_qkv_bias = lax.dynamic_slice_in_dim(
        full_qkv_bias.reshape(3, head_count, head_dim), model_rank * local_heads, local_heads, 1
    ).reshape(3 * local_width)
    local_up_bias = lax.dynamic_slice_in_dim(
        full_up_bias, model_rank * hidden_local, hidden_local, 0
    )
    token_rows = token_rows.reshape(group_rows, 2 * model_width)
    normed_rows = token_rows[:, :model_width].astype(f32)
    grad_rows = token_rows[:, model_width:]
    h_attn = (normed_rows * gain_one + shift_one).astype(bf16)
    h_mlp = (normed_rows * gain_two + shift_two).astype(bf16)

    group_index = fsdp_rank * group_rows + jnp.arange(group_rows, dtype=jnp.int32)
    group_seg, group_pos = token_segments(seq_lengths, group_index)
    group_cos, group_sin = rotary_tables(group_pos)
    causal_mask = (
        jnp.arange(group_rows, dtype=jnp.int32)[None, :]
        <= jnp.arange(group_rows, dtype=jnp.int32)[:, None]
    )
    projected = jnp.dot(h_attn, w_qkv, preferred_element_type=f32) + local_qkv_bias[None, :]
    projected = projected.reshape(group_rows, 3, local_heads, head_dim)
    query_rows = rotate(projected[:, 0], group_cos, group_sin).astype(bf16)
    own_keys = rotate(projected[:, 1], group_cos, group_sin).astype(bf16)
    own_pair = jnp.concatenate(
        [own_keys.reshape(group_rows, local_width),
         projected[:, 2].astype(bf16).reshape(group_rows, local_width)], axis=1
    )
    (others,) = call(
        functools.partial(keys_kernel, chip_count, hops),
        1,
        (own_pair,),
        [((hops + 1, 2) + own_pair.shape, bf16)],
        [anywhere],
        [anywhere],
        [],
        1 + 2 * hops,
        0,
    )

    pre_act = jnp.dot(h_mlp, w_up, preferred_element_type=f32) + local_up_bias[None, :]
    activation = gelu_value(pre_act).astype(bf16)
    mlp_part = contract_cols(activation, w_down)
    hidden_grads = jnp.dot(grad_rows, w_down, preferred_element_type=f32) * gelu_slope(pre_act)
    hidden_low = hidden_grads.astype(bf16)
    mlp_input_part = contract_cols(hidden_low, w_up)

    key_sets = [(own_pair, group_seg, True, None)]
    for step in range(hops + 1):
        for side in range(2):
            source = (chip - step) * 2 + side
            if step == 0:
                if side == 1:
                    continue
                valid = core == 1
            else:
                valid = source >= 0
            pair = others[step, side]
            earlier = source * group_rows + jnp.arange(group_rows, dtype=jnp.int32)
            earlier_seg, unused = token_segments(seq_lengths, earlier)
            earlier_seg = jnp.where(valid, earlier_seg, -1)
            key_sets.append((pair, earlier_seg, False, (step, side)))

    def is_live(key_segs):
        return key_segs[-1] == group_seg[0]

    def block_scores(pair, key_segs, causal):
        key_block = pair[:, :local_width].reshape(group_rows, local_heads, head_dim)
        scores = (
            jnp.einsum("qhd,khd->hqk", query_rows, key_block, preferred_element_type=f32)
            * score_scale
        )
        key_mask = group_seg[:, None] == key_segs[None, :]
        if causal:
            key_mask = key_mask & causal_mask
        return (scores, key_mask[None])

    def stats_update(carried_state, pair, key_segs):
        row_top, row_total = carried_state
        scores, key_mask = block_scores(pair, key_segs, False)
        masked = jnp.where(key_mask, scores, NEG_FILL)
        new_top = jnp.maximum(row_top, jnp.max(masked, axis=-1))
        new_total = row_total * jnp.exp(row_top - new_top) + jnp.sum(
            jnp.where(key_mask, jnp.exp(masked - new_top[..., None]), 0.0), axis=-1
        )
        return (new_top, new_total)

    scores, key_mask = block_scores(own_pair, group_seg, True)
    masked = jnp.where(key_mask, scores, NEG_FILL)
    row_top = jnp.max(masked, axis=-1)
    row_total = jnp.sum(jnp.where(key_mask, jnp.exp(masked - row_top[..., None]), 0.0), axis=-1)
    for pair, key_segs, causal, slot in key_sets[1:]:
        row_top, row_total = lax.cond(
            is_live(key_segs),
            lambda carried_state: stats_update(carried_state, pair, key_segs),
            lambda carried_state: carried_state,
            (row_top, row_total),
        )
    row_lse = row_top + jnp.log(row_total)

    def block_output(pair, key_segs, causal):
        scores, key_mask = block_scores(pair, key_segs, causal)
        attn_probs = jnp.where(key_mask, jnp.exp(scores - row_lse[..., None]), 0.0).astype(bf16)
        value_block = pair[:, local_width:].reshape(group_rows, local_heads, head_dim)
        return jnp.einsum("hqk,khd->qhd", attn_probs, value_block, preferred_element_type=f32)

    zero_heads = jnp.zeros((group_rows, local_heads, head_dim), f32)
    mixed = block_output(own_pair, group_seg, True)
    for pair, key_segs, causal, slot in key_sets[1:]:
        mixed = mixed + lax.cond(
            is_live(key_segs), lambda: block_output(pair, key_segs, False), lambda: zero_heads
        )
    out_heads = mixed.astype(bf16)
    out_flat = out_heads.reshape(group_rows, local_width)
    branch_part = (mlp_part + contract_cols(out_flat, w_dense)).astype(bf16)
    head_grads = (
        jnp.dot(grad_rows, w_dense, preferred_element_type=f32)
        .astype(bf16)
        .reshape(group_rows, local_heads, head_dim)
    )
    row_delta = jnp.sum(head_grads.astype(f32) * out_heads.astype(f32), axis=-1).T

    def block_grads(pair, key_segs, causal):
        scores, key_mask = block_scores(pair, key_segs, causal)
        attn_probs = jnp.where(key_mask, jnp.exp(scores - row_lse[..., None]), 0.0)
        key_block = pair[:, :local_width].reshape(group_rows, local_heads, head_dim)
        value_block = pair[:, local_width:].reshape(group_rows, local_heads, head_dim)
        prob_grads = jnp.einsum(
            "qhd,khd->hqk", head_grads, value_block, preferred_element_type=f32
        )
        score_grads = (attn_probs * (prob_grads - row_delta[..., None]) * score_scale).astype(bf16)
        query_grads = jnp.einsum(
            "hqk,khd->qhd", score_grads, key_block, preferred_element_type=f32
        )
        key_part = jnp.einsum(
            "hqk,qhd->khd", score_grads, query_rows, preferred_element_type=f32
        )
        value_part = jnp.einsum(
            "hqk,qhd->khd", attn_probs.astype(bf16), head_grads, preferred_element_type=f32
        )
        return (
            query_grads,
            jnp.concatenate(
                [
                    key_part.reshape(group_rows, local_width),
                    value_part.reshape(group_rows, local_width),
                ],
                axis=1,
            ).astype(bf16),
        )

    zero_pair = jnp.zeros((group_rows, 2 * local_width), bf16)
    query_grads, own_part = block_grads(own_pair, group_seg, True)
    parts = {}
    for pair, key_segs, causal, slot in key_sets[1:]:
        query_part, parts[slot] = lax.cond(
            is_live(key_segs),
            lambda: block_grads(pair, key_segs, False),
            lambda: (zero_heads, zero_pair),
        )
        query_grads = query_grads + query_part
    pair_part = parts[(0, 0)]
    first = core == 0
    near_parts = [jnp.where(first, own_part, pair_part), jnp.where(first, zero_pair, own_part)]
    part_stack = jnp.stack(
        [
            jnp.stack([near_parts[side]] + [parts[(step, side)] for step in range(1, hops + 1)])
            for side in range(2)
        ]
    )
    branch_stack = branch_part.reshape(model_count, tok_dev, model_width)
    block_shape = own_pair.shape
    pair_grads, branch_rows = call(
        functools.partial(pair_kernel, chip_count, model_count, hops),
        2,
        (part_stack, branch_stack),
        [(block_shape, f32), (branch_stack.shape, bf16)],
        [vmem, anywhere],
        [vmem, anywhere],
        [
            pltpu.VMEM((hops + 1,) + block_shape, bf16),
            pltpu.VMEM((hops,) + block_shape, bf16),
            pltpu.VMEM((hops,) + block_shape, bf16),
        ],
        2 * hops + 1 + model_count - 1,
        1,
    )
    layer_output = (
        layer_input
        + jnp.sum(branch_rows.astype(f32), axis=0)
        + (full_dense_bias + full_down_bias)[None, :]
    )
    key_grads = rotate_back(
        pair_grads[:, :local_width].reshape(group_rows, local_heads, head_dim),
        group_cos,
        group_sin,
    )
    query_back = rotate_back(query_grads, group_cos, group_sin)
    qkv_grads = jnp.concatenate(
        [
            query_back.reshape(group_rows, local_width),
            key_grads.reshape(group_rows, local_width),
            pair_grads[:, local_width:],
        ],
        axis=1,
    ).astype(bf16)
    grad_parts = jnp.concatenate(
        [
            contract_rows(h_attn, qkv_grads).astype(bf16),
            contract_rows(grad_rows, out_flat).astype(bf16),
            contract_rows(h_mlp, hidden_low).astype(bf16),
            contract_rows(grad_rows, activation).astype(bf16),
        ],
        axis=1,
    ).reshape(chip_count, 2, owned, columns)
    attn_input_part = contract_cols(qkv_grads, w_qkv)
    hat_part = (attn_input_part * gain_one + mlp_input_part * gain_two).astype(bf16)
    hat_stack = hat_part.reshape(model_count, tok_dev, model_width)

    def widen(vector, shape, axis, offset):
        return lax.dynamic_update_slice_in_dim(
            jnp.zeros(shape, f32), vector, offset, axis
        ).reshape(fsdp_count, -1)

    qkv_bias_part = jnp.sum(qkv_grads.astype(f32), axis=0)
    small = [
        widen(
            qkv_bias_part.reshape(3, local_heads, head_dim),
            (3, head_count, head_dim),
            1,
            model_rank * local_heads,
        ),
        jnp.sum(cotangent, axis=0).reshape(fsdp_count, -1),
        widen(jnp.sum(hidden_grads, axis=0), (hidden_total,), 0, model_rank * hidden_local),
        jnp.sum(attn_input_part * normed_rows, axis=0).reshape(fsdp_count, -1),
        jnp.sum(attn_input_part, axis=0).reshape(fsdp_count, -1),
        jnp.sum(mlp_input_part * normed_rows, axis=0).reshape(fsdp_count, -1),
        jnp.sum(mlp_input_part, axis=0).reshape(fsdp_count, -1),
    ]
    small_pack = jnp.concatenate(small, axis=1)
    small_width = small_pack.shape[1]
    small_pack = small_pack.reshape(chip_count, 2, 1, small_width)
    grad_shape, small_shape = (owned, columns), (1, small_width)
    grads, small_sums, hat_rows = call(
        functools.partial(close_kernel, chip_count, model_count),
        3,
        (grad_parts, small_pack, hat_stack),
        [(grad_shape, f32), (small_shape, f32), (hat_stack.shape, bf16)],
        [vmem, vmem, anywhere],
        [vmem, vmem, anywhere],
        [
            pltpu.VMEM((chip_count,) + grad_shape, bf16),
            pltpu.VMEM((chip_count - 1,) + grad_shape, bf16),
            pltpu.VMEM((chip_count - 1,) + grad_shape, bf16),
            pltpu.VMEM((chip_count,) + small_shape, f32),
            pltpu.VMEM((chip_count - 1,) + small_shape, f32),
            pltpu.VMEM((chip_count - 1,) + small_shape, f32),
        ],
        2 * (2 * chip_count - 1) + model_count - 1,
        1,
    )
    heavy = grads[:, : 4 * local_width].astype(bf16)
    heavy_all, small_all = call(
        functools.partial(last_kernel, model_count),
        4,
        (heavy, small_sums),
        [((model_count,) + heavy.shape, bf16), ((model_count,) + small_shape, f32)],
        [anywhere] * 2,
        [anywhere] * 2,
        [],
        2 * (model_count - 1),
        2,
    )
    grad_hat = jnp.sum(hat_rows.astype(f32), axis=0)
    input_grad = cotangent + norm_back(grad_hat, normed, inv_std)
    heavy_all = heavy_all.astype(f32)
    grad_qkv_w = (
        heavy_all[:, :, : 3 * local_width]
        .reshape(model_count, owned, 3, local_heads, head_dim)
        .transpose(1, 2, 0, 3, 4)
        .reshape(owned, 3, head_count, head_dim)
    )
    grad_dense_w = (
        heavy_all[:, :, 3 * local_width :].transpose(0, 2, 1).reshape(model_width, owned)
    )
    small_total = jnp.sum(small_all, axis=0)[0]
    final = []
    at = 0
    for piece in small:
        final.append(small_total[at : at + piece.shape[1]])
        at += piece.shape[1]
    return (
        layer_output,
        input_grad,
        grad_qkv_w,
        final[0],
        grad_dense_w,
        final[1],
        final[3],
        final[4],
        final[5],
        final[6],
        grads[:, 4 * local_width : 4 * local_width + hidden_local],
        final[2],
        grads[:, 4 * local_width + hidden_local :],
        final[1],
    )


def solution(mesh):
    placed = (
        P(("fsdp", "mp"), None),
        P(("fsdp", "mp"), None),
        P(),
        P("fsdp"),
        P("fsdp"),
        P("fsdp"),
        P("fsdp"),
        P("fsdp", None, None, None),
        P("fsdp"),
        P(None, "fsdp"),
        P("fsdp"),
        P("fsdp", "mp"),
        P("fsdp"),
        P("fsdp", "mp"),
        P("fsdp"),
    )
    return jax.shard_map(
        on_device,
        mesh=mesh,
        in_specs=placed,
        out_specs=(
            P(("fsdp", "mp"), None),
            P(("fsdp", "mp"), None),
            P("fsdp", None, None, None),
            P("fsdp"),
            P(None, "fsdp"),
            P("fsdp"),
            P("fsdp"),
            P("fsdp"),
            P("fsdp"),
            P("fsdp"),
            P("fsdp", "mp"),
            P("fsdp"),
            P("fsdp", "mp"),
            P("fsdp"),
        ),
        check_vma=False,
    )
```

time: 627 us -> 345 us (0.55); the launches traced: 617 us -> 349 us
  waiting for transfers between devices: 284 us -> 0 us
  Pallas kernels: 0 us -> 226 us
  blocking collectives: 151 us -> 0 us
  starting transfers between devices: 38.1 us -> 0 us
  between operations: 24.1 us -> 8.61 us
  local copies, waits for them, and re-layouts: 57.7 us -> 50.4 us
    pallas_call x0 -> x5, Pallas kernels: none -> 226 us  [call(): pl.pallas_call(kernel, out_shape=[jax.ShapeDtypeStruct(shape, dtype) for...]
    all_gather x3 -> x0, blocking collectives: 88.1 us -> none  [the longest x1 52.3 us: on_device(): lax.all_gather(up_bias, 'fsdp', axis=0, tiled=True)]
    reduce_scatter x3 -> x0, waiting for transfers between devices: 84.7 us -> none  [the longest x1 41.2 us: on_device(): lax.psum_scatter(grad_up_w, 'fsdp', scatter_dimension=0, tiled=True)]
    unnamed x12 -> x0, waiting for transfers between devices: 82.1 us -> none
    unnamed x2 -> x0, blocking collectives: 52.4 us -> none
    all_to_all x3 -> x0, waiting for transfers between devices: 34.5 us -> none  [the longest x1 18.9 us: on_device(): lax.all_to_all(stacked, 'mp', split_axis=2, concat_axis=0, tiled=True)]
    psum x1 -> x0, waiting for transfers between devices: 30.6 us -> none  [on_device(): lax.psum((reduced[0], reduced[1], reduced[2], reduced[3], reduced[4], red...]
    all_gather x4 -> x0, waiting for transfers between devices: 28.5 us -> none  [the longest x1 28.4 us: on_device(): lax.all_gather(qkv_weight, 'fsdp', axis=0, tiled=True)]
  transfers between devices with their start and end apart: 21 -> 0, of which waited for: 12 -> 0; matrix products, arithmetic and copies ran while one was open for 17% -> 0% of each run, Pallas kernels for 0% -> 0%
where the time goes in v1:
time: 345 us; the launch traced here: 349 us
  Pallas kernels  226 us (66%)
  local copies, waits for them, and re-layouts  50.4 us (15%)
  matrix products  38.8 us (11%)
  other arithmetic  24.3 us (7%)
  between operations  8.61 us (2%)
    pallas_call x5, Pallas kernels, call(): pl.pallas_call(kernel, out_shape=[jax.ShapeDtypeStruct(shape, dtype) for...  226 us
    dot_general x4, matrix products, contract_cols(): lax.dot_general(left, right, (((1,), (1,)), ((), ())), preferred_element_...  10.1 us
    broadcast_in_dim x10, local copies, waits for them, and re-layouts, on_device(): zero_heads = jnp.zeros((group_rows, local_heads, head_dim), f32)  8.03 us

profile of v1, /device:TPU:0, one launch (start us, length us, event | category | flops | bytes accessed | tf_op | source)
XLA Modules:
  0.0 349.1 jit_solution(10074357526747149228)
XLA Ops:
  3.6 1.0 dynamic-slice_bitcast_fusion
  4.6 1.9 concatenate.149.w_ref
  6.4 1.1 reduce_sum.254
  7.6 1.2 multiply_reduce_fusion.2
  8.8 1.9 fusion.138
  12.3 33.9 %shard_map.254 = (bf16[8,96,2304]{2,1,0:T(8,128)(2,1)}, f32[8,1,1248]{2,1,0:T(1,128)}, bf16[4,128,1536]{2,1,0:T(8,128)(2,1)}) custom-call(bf16[96,2304]{1,0:T(8,128)(2,1)} %concatenate.149.w_ref, f32[1,1248]{1,0:T(1,128)} %convert_element_type.243.v_ref, bf16[128,1536]{1,0:T(8,128)(2,1)} %pad_maximum_fusion.8.t_ref), custom_call_target="tpu_custom_call" | custom-call | tf_op jit(solution)/shard_map/pallas_call | solution.py:353
  47.1 1.5 add_reduce_fusion
  48.8 2.1 convolution_add_fusion.1
  52.2 1.4 select_reduce_fusion.5
  54.6 1.0 slice.497
  56.4 1.9 pad_maximum_fusion.9.x_ref
  58.4 18.2 %shard_map.255 = bf16[3,2,512,384]{3,2,1,0:T(8,128)(2,1)} custom-call(bf16[512,384]{1,0:T(8,128)(2,1)} %pad_maximum_fusion.9.x_ref), custom_call_target="tpu_custom_call" | custom-call | tf_op jit(solution)/shard_map/pallas_call | solution.py:353
  76.5 2.8 slice_bitcast_fusion.4
  89.4 1.3 slice.305
  95.8 1.3 conditional.24
  97.1 2.5 convolution_convert_fusion.11
  99.7 3.9 %multiply_reduce_fusion.1 = (f32[512,3]{0,1:T(4,128)}, bf16[512,3,64]{0,2,1:T(8,128)(2,1)}) fusion(bf16[512,3,64]{0,2,1:T(8,128)(2,1)} %bitcast.82, f32[512,3,64]{0,2,1:T(8,128)} %get-tuple-element.933, f32[512,3,64]{0,2,1:T(8,128)} %get-tuple-element.932, f32[512,3,64]{0,2,1:T(8,128)} %get-tuple-element.931, f32[512,3,64]{0,2,1:T(8,128)} %get-tuple-element.930, ...), kind=kOutput, calls=%fused_computation.201 | convolution fusion | flops 104790528 | bytes 5978112 | tf_op jit(solution)/shard_map/hqk,khd->qhd/dot_general | solution.py:546
  103.5 1.6 conditional.25
  105.2 1.6 conditional.26
  106.8 1.7 conditional.27
  108.5 3.6 %multiply_convert_fusion.5 = bf16[3,512,512]{1,2,0:T(8,128)(2,1)} fusion(f32[3,512,512]{1,2,0:T(8,128)S(1)} %get-tuple-element.844, bf16[512,3,64]{0,2,1:T(8,128)(2,1)} %bitcast.82, f32[3,512]{1,0:T(4,128)} %bitcast.344, f32[3,512]{1,0:T(4,128)} %log_add_fusion, pred[512,512]{0,1:T(8,128)(4,1)} %copy-done.10, f32[512,3,3,64]{0,3,2,1:T(8,128)} %bitcast.286), kind=kOutput, calls=%fused_computation.116 | convolution fusion | flops 106168320 | bytes 5390336 | tf_op jit(solution)/shard_map/qhd,khd->hqk/dot_general | solution.py:569
  112.1 1.6 conditional.28
  113.6 1.6 conditional.29
  115.2 2.5 fusion.89
  119.2 2.8 fusion.113
  122.9 3.7 %multiply_convert_fusion.6 = (bf16[512,768]{1,0:T(8,128)(2,1)S(1)}, f32[512,768]{1,0:T(8,128)}) fusion(f32[768]{0:T(1024)S(1)} %dynamic_slice.15, bf16[768,2304]{1,0:T(8,128)(2,1)} %bitcast.335, f32[768]{0:T(1024)S(1)} %add.267, f32[768]{0:T(1024)S(1)} %mul.404, bf16[512,1536]{1,0:T(8,128)(2,1)} %bitcast.356), kind=kOutput, calls=%fused_computation.143 | convolution fusion | flops 607911936 | bytes 4334592 | tf_op jit(solution)/shard_map/dot_general | solution.py:482
  126.7 3.3 add_convert_fusion.1
  131.5 2.5 convolution_convert_fusion.9
  134.0 1.1 copy.173
  135.1 1.1 fusion.110
  136.3 1.3 maximum_bitcast_fusion
  138.0 1.3 maximum_bitcast_fusion.1
  139.3 1.7 pad_maximum_fusion.6.p_ref
  141.0 114.7 %shard_map.256 = (f32[512,384]{1,0:T(8,128)}, bf16[4,128,768]{2,1,0:T(8,128)(2,1)}) custom-call(bf16[2,3,512,384]{3,2,1,0:T(8,128)(2,1)} %pad_maximum_fusion.6.p_ref, bf16[4,128,768]{2,1,0:T(8,128)(2,1)} %bitcast.299), custom_call_target="tpu_custom_call" | custom-call | tf_op jit(solution)/shard_map/pallas_call | solution.py:353
  255.7 1.1 slice.329
  258.2 1.3 slice.496
  259.5 2.0 fusion.99
  261.6 2.5 fusion.139
  264.2 2.0 fusion.126
  269.4 2.0 convolution_convert_fusion.6
  272.6 4.0 %copy.190 = bf16[768,2304]{1,0:T(8,128)(2,1)} copy(bf16[768,2304]{0,1:T(8,128)(2,1)S(1)} %pad_maximum_fusion.5) | data formatting | bytes 7077888 | tf_op jit(solution)/shard_map/concatenate | solution.py:648
  276.6 44.5 %shard_map.257 = (f32[96,2304]{1,0:T(8,128)}, f32[1,1152]{1,0:T(1,128)}, bf16[4,128,768]{2,1,0:T(8,128)(2,1)}) custom-call(bf16[4,2,96,2304]{3,2,1,0:T(8,128)(2,1)} %bitcast.269, f32[4,2,1,1152]{3,2,1,0:T(1,128)} %concatenate.178.v_ref, bf16[4,128,768]{2,1,0:T(8,128)(2,1)} %bitcast.292), custom_call_target="tpu_custom_call" | custom-call | tf_op jit(solution)/shard_map/pallas_call | solution.py:353
  321.0 1.6 slice.498.g_ref
  322.7 14.8 %shard_map.258 = (bf16[4,96,768]{2,1,0:T(8,128)(2,1)}, f32[4,1,1152]{2,1,0:T(1,128)}) custom-call(bf16[96,768]{1,0:T(8,128)(2,1)} %slice.498.g_ref, f32[1,1152]{1,0:T(1,128)} %get-tuple-element.390.v_ref), custom_call_target="tpu_custom_call" | custom-call | tf_op jit(solution)/shard_map/pallas_call | solution.py:353
  337.5 1.2 slice.401
  339.1 1.1 copy.192
  343.6 1.5 convert_reduce_fusion
  346.4 1.9 fusion.137
  (251 shorter events, 44.3 us)
Async XLA Ops:
  0.6 2.8 copy-start
  0.7 10.8 %copy-start.71 = (bf16[288]{0:T(512)(128)(2,1)S(1)}, bf16[288]{0:T(512)(128)(2,1)}, u32[]{:S(2)}) copy-start(bf16[288]{0:T(512)(128)(2,1)} %param.53) | copy-start | bytes 1732
  0.7 10.8 %copy-start.72 = (bf16[384]{0:T(512)(128)(2,1)S(1)}, bf16[384]{0:T(512)(128)(2,1)}, u32[]{:S(2)}) copy-start(bf16[384]{0:T(512)(128)(2,1)} %param.57) | copy-start | bytes 2308
  0.7 10.8 %copy-start.73 = (bf16[96]{0:T(256)(128)(2,1)S(1)}, bf16[96]{0:T(256)(128)(2,1)}, u32[]{:S(2)}) copy-start(bf16[96]{0:T(256)(128)(2,1)} %param.55) | copy-start | bytes 580
  0.7 10.8 %copy-start.74 = (bf16[96]{0:T(256)(128)(2,1)S(1)}, bf16[96]{0:T(256)(128)(2,1)}, u32[]{:S(2)}) copy-start(bf16[96]{0:T(256)(128)(2,1)} %param.59) | copy-start | bytes 580
  0.7 10.8 %copy-start.75 = (bf16[96]{0:T(256)(128)(2,1)S(1)}, bf16[96]{0:T(256)(128)(2,1)}, u32[]{:S(2)}) copy-start(bf16[96]{0:T(256)(128)(2,1)} %param.48) | copy-start | bytes 580
  0.7 10.8 %copy-start.76 = (bf16[96]{0:T(256)(128)(2,1)S(1)}, bf16[96]{0:T(256)(128)(2,1)}, u32[]{:S(2)}) copy-start(bf16[96]{0:T(256)(128)(2,1)} %param.49) | copy-start | bytes 580
  0.7 10.8 %copy-start.77 = (bf16[96]{0:T(256)(128)(2,1)S(1)}, bf16[96]{0:T(256)(128)(2,1)}, u32[]{:S(2)}) copy-start(bf16[96]{0:T(256)(128)(2,1)} %param.50) | copy-start | bytes 580
  0.7 10.8 %copy-start.78 = (bf16[96]{0:T(256)(128)(2,1)S(1)}, bf16[96]{0:T(256)(128)(2,1)}, u32[]{:S(2)}) copy-start(bf16[96]{0:T(256)(128)(2,1)} %param.51) | copy-start | bytes 580
  3.4 47.7 %copy-start.29 = (f32[512,8]{0,1:T(8,128)}, f32[512,8]{0,1:T(8,128)S(1)}, u32[]{:S(2)}) copy-start(f32[512,8]{0,1:T(8,128)S(1)} %get-tuple-element.839) | copy-start | bytes 49156
  3.4 47.7 %copy-start.31 = (f32[512,8]{0,1:T(8,128)}, f32[512,8]{0,1:T(8,128)S(1)}, u32[]{:S(2)}) copy-start(f32[512,8]{0,1:T(8,128)S(1)} %get-tuple-element.840) | copy-start | bytes 49156
  7.5 43.4 %copy-start.63 = (f32[128]{0:T(128)}, f32[128]{0:T(128)S(1)}, u32[]{:S(2)}) copy-start(f32[128]{0:T(128)S(1)} %broadcast_multiply_fusion.2) | copy-start | bytes 1540
  8.8 42.2 %copy-start.65 = (f32[128]{0:T(128)}, f32[128]{0:T(128)S(1)}, u32[]{:S(2)}) copy-start(f32[128]{0:T(128)S(1)} %add_rsqrt_fusion) | copy-start | bytes 1540
  48.7 2.6 copy-start.67
  51.0 2.6 copy-start.33
  58.4 21.0 %copy-start.61 = (s32[512]{0:T(512)S(1)}, s32[512]{0:T(512)}, u32[]{:S(2)}) copy-start(s32[512]{0:T(512)} %get-tuple-element.774) | copy-start | bytes 6148
  58.4 21.0 %copy-start.62 = (s32[512]{0:T(512)S(1)}, s32[512]{0:T(512)}, u32[]{:S(2)}) copy-start(s32[512]{0:T(512)} %get-tuple-element.777) | copy-start | bytes 6148
  58.4 23.4 %copy-start.28 = (f32[3,512]{1,0:T(4,128)S(1)}, f32[3,512]{1,0:T(4,128)}, u32[]{:S(2)}) copy-start(f32[3,512]{1,0:T(4,128)} %select_reduce_fusion.5) | copy-start | bytes 18436
  84.4 3.8 %copy-start.40 = (s32[512]{0:T(512)}, s32[512]{0:T(512)S(1)}, u32[]{:S(2)}) copy-start(s32[512]{0:T(512)S(1)} %get-tuple-element.853) | copy-start | bytes 6148
  115.2 3.9 %copy-start.23 = (bf16[512,3,64]{0,2,1:T(8,128)(2,1)S(1)}, bf16[512,3,64]{0,2,1:T(8,128)(2,1)}, u32[]{:S(2)}) copy-start(bf16[512,3,64]{0,2,1:T(8,128)(2,1)} %get-tuple-element.846) | copy-start | bytes 589828
  115.2 7.5 %copy-start.52 = (f32[8,96]{1,0:T(8,128)S(1)}, f32[8,96]{1,0:T(8,128)}, u32[]{:S(2)}) copy-start(f32[8,96]{1,0:T(8,128)} %get-tuple-element.771) | copy-start | bytes 9220
  115.2 7.6 %copy-start.51 = (f32[8,96]{1,0:T(8,128)S(1)}, f32[8,96]{1,0:T(8,128)}, u32[]{:S(2)}) copy-start(f32[8,96]{1,0:T(8,128)} %get-tuple-element.770) | copy-start | bytes 9220
  122.9 3.8 %copy-start.17 = (f32[512,768]{1,0:T(8,128)S(1)}, f32[512,768]{1,0:T(8,128)}, u32[]{:S(2)}) copy-start(f32[512,768]{1,0:T(8,128)} %fusion.113) | copy-start | bytes 4718596
  126.6 4.0 %copy-start.81 = (bf16[512,768]{1,0:T(8,128)(2,1)}, bf16[512,768]{1,0:T(8,128)(2,1)S(1)}, u32[]{:S(2)}) copy-start(bf16[512,768]{1,0:T(8,128)(2,1)S(1)} %get-tuple-element.841) | copy-start | bytes 2359300
  126.7 3.3 copy-start.3
  126.7 3.3 copy-start.21
  126.7 3.3 copy-start.34
  126.7 3.3 copy-start.36
  126.7 4.8 %copy-start.42 = (f32[3,512]{1,0:T(4,128)S(1)}, f32[3,512]{1,0:T(4,128)}, u32[]{:S(2)}) copy-start(f32[3,512]{1,0:T(4,128)} %log_add_fusion) | copy-start | bytes 18436
  134.0 3.7 %copy-start.25 = (bf16[3,64,512]{2,1,0:T(8,128)(2,1)S(1)}, bf16[3,64,512]{2,1,0:T(8,128)(2,1)}, u32[]{:S(2)}) copy-start(bf16[3,64,512]{2,1,0:T(8,128)(2,1)} %convolution_convert_fusion.9) | copy-start | bytes 589828
  140.9 116.0 %copy-start.30 = (f32[512,8]{0,1:T(8,128)S(1)}, f32[512,8]{0,1:T(8,128)}, u32[]{:S(2)}) copy-start(f32[512,8]{0,1:T(8,128)} %copy-done.29) | copy-start | bytes 49156
  141.0 116.0 %copy-start.32 = (f32[512,8]{0,1:T(8,128)S(1)}, f32[512,8]{0,1:T(8,128)}, u32[]{:S(2)}) copy-start(f32[512,8]{0,1:T(8,128)} %copy-done.31) | copy-start | bytes 49156
  141.0 116.9 %copy-start.27 = (bf16[512,3,48]{0,2,1:T(8,128)(2,1)S(1)}, bf16[512,3,48]{0,2,1:T(8,128)(2,1)}, u32[]{:S(2)}) copy-start(bf16[512,3,48]{0,2,1:T(8,128)(2,1)} %slice.500) | copy-start | bytes 442372
  257.8 3.7 %copy-start.80 = (bf16[4,128,1536]{2,1,0:T(8,128)(2,1)S(1)}, bf16[4,128,1536]{2,1,0:T(8,128)(2,1)}, u32[]{:S(2)}) copy-start(bf16[4,128,1536]{2,1,0:T(8,128)(2,1)} %get-tuple-element.363) | copy-start | bytes 4718596
  258.2 3.4 copy-start.39
  264.1 3.2 copy-start.49
  264.1 4.0 %copy-start.70 = (f32[768]{0:T(1024)S(1)}, f32[768]{0:T(1024)}, u32[]{:S(2)}) copy-start(f32[768]{0:T(1024)} %copy-done.69) | copy-start | bytes 9220
  266.1 2.9 copy-start.24
  337.5 2.7 copy-start.9
  339.1 2.6 copy-start.48
  340.2 4.8 %copy-start.2 = (f32[128,768]{1,0:T(8,128)S(1)}, f32[128,768]{1,0:T(8,128)}, u32[]{:S(2)}) copy-start(f32[128,768]{1,0:T(8,128)} %param.45) | copy-start | bytes 1179652
  340.2 4.8 %copy-start.64 = (f32[128]{0:T(128)S(1)}, f32[128]{0:T(128)}, u32[]{:S(2)}) copy-start(f32[128]{0:T(128)} %copy-done.63) | copy-start | bytes 1540
  340.2 4.8 %copy-start.66 = (f32[128]{0:T(128)S(1)}, f32[128]{0:T(128)}, u32[]{:S(2)}) copy-start(f32[128]{0:T(128)} %copy-done.65) | copy-start | bytes 1540
  340.2 5.1 %copy-start.26 = (bf16[4,128,768]{2,1,0:T(8,128)(2,1)S(1)}, bf16[4,128,768]{2,1,0:T(8,128)(2,1)}, u32[]{:S(2)}) copy-start(bf16[4,128,768]{2,1,0:T(8,128)(2,1)} %get-tuple-element.381) | copy-start | bytes 2359300
  340.3 5.1 %copy-start.50 = (f32[8,96]{1,0:T(8,128)S(1)}, f32[8,96]{1,0:T(8,128)}, u32[]{:S(2)}) copy-start(f32[8,96]{1,0:T(8,128)} %get-tuple-element.769) | copy-start | bytes 9220
  340.3 5.1 %copy-start.18 = (f32[128,768]{1,0:T(8,128)S(1)}, f32[128,768]{1,0:T(8,128)}, u32[]{:S(2)}) copy-start(f32[128,768]{1,0:T(8,128)} %param.46) | copy-start | bytes 1179652
  342.4 5.9 %copy-start.79 = (f32[96]{0:T(128)}, f32[96]{0:T(128)S(1)}, u32[]{:S(2)}) copy-start(f32[96]{0:T(128)S(1)} %get-tuple-element.923) | copy-start | bytes 1156
  343.6 5.3 %copy-start.1 = (bf16[96,3,12,64]{0,3,2,1:T(8,128)(2,1)S(1)}, bf16[96,3,12,64]{0,3,2,1:T(8,128)(2,1)}, u32[]{:S(2)}) copy-start(bf16[96,3,12,64]{0,3,2,1:T(8,128)(2,1)} %param.52) | copy-start | bytes 1327108
  (16 other events, 29.7 us)

commit v2 on v1

--- a/solution.py
+++ b/solution.py
@@ -347,6 +347,119 @@
     started += model_exchange(copies, g_ref, g_out, model_count, True)
     for copy in started:
         copy.wait()
+
+
+def over_rows(left, right):
+    return lax.dot_general(
+        left, right, (((0,), (0,)), ((), ())), preferred_element_type=jnp.float32
+    )
+
+
+def attention_kernel(
+    heads, slots, live, q_ref, own_ref, others, h_ref, q_seg, own_seg, key_segs,
+    out, q_grads, parts, tops, totals, mixed, lse, delta,
+):
+    rows, width = q_ref.shape
+    head_dim = width // heads
+    core = lax.axis_index("fsdp") % 2
+    scale = jnp.asarray(1.0 / math.sqrt(head_dim), jnp.bfloat16)
+
+    def columns(value, head, base=0):
+        return value[:, base + head * head_dim : base + (head + 1) * head_dim]
+
+    def lines(head):
+        return slice(head * head_dim, (head + 1) * head_dim)
+
+    queries = q_ref[...] * scale
+    upper = h_ref[...]
+    query_segs = q_seg[...]
+    own_mask = (own_seg[...] == query_segs) & (
+        lax.broadcasted_iota(jnp.int32, (rows, rows), 0)
+        <= lax.broadcasted_iota(jnp.int32, (rows, rows), 1)
+    )
+
+    def scores_of(block, mask, head):
+        return jnp.where(
+            mask, contract_cols(columns(block, head), columns(queries, head)), NEG_FILL
+        )
+
+    own = own_ref[...]
+    for head in range(heads):
+        scores = scores_of(own, own_mask, head)
+        top = jnp.max(scores, axis=0, keepdims=True)
+        weights = jnp.exp(scores - top)
+        tops[head] = top
+        totals[head] = jnp.sum(weights, axis=0, keepdims=True)
+        mixed[lines(head)] = over_rows(
+            columns(own, head, width), weights.astype(jnp.bfloat16)
+        )
+
+    def forward_slot(index, carried):
+        @pl.when(live[index] == 1)
+        def _():
+            block = others[index]
+            mask = key_segs[index] == query_segs
+            for head in range(heads):
+                scores = scores_of(block, mask, head)
+                top = jnp.maximum(tops[head], jnp.max(scores, axis=0, keepdims=True))
+                shrink = jnp.exp(tops[head] - top)
+                weights = jnp.exp(scores - top)
+                tops[head] = top
+                totals[head] = totals[head] * shrink + jnp.sum(weights, axis=0, keepdims=True)
+                mixed[lines(head)] = mixed[lines(head)] * shrink + over_rows(
+                    columns(block, head, width), weights.astype(jnp.bfloat16)
+                )
+
+        return carried
+
+    lax.fori_loop(0, slots, forward_slot, 0)
+    upper_lines = upper.astype(jnp.float32).T
+    for head in range(heads):
+        result = (mixed[lines(head)] / totals[head]).astype(jnp.bfloat16).astype(jnp.float32)
+        mixed[lines(head)] = result
+        lse[head] = tops[head] + jnp.log(totals[head])
+        delta[head] = jnp.sum(result * upper_lines[lines(head)], axis=0, keepdims=True)
+    out[...] = mixed[...].T.astype(jnp.bfloat16)
+
+    def grads_of(block, mask):
+        key_parts, value_parts, query_parts = [], [], []
+        for head in range(heads):
+            probs = jnp.exp(scores_of(block, mask, head) - lse[head])
+            prob_grads = contract_cols(columns(block, head, width), columns(upper, head))
+            score_grads = (probs * (prob_grads - delta[head])).astype(jnp.bfloat16)
+            query_parts.append(over_rows(columns(block, head), score_grads))
+            key_parts.append(
+                jnp.dot(score_grads, columns(queries, head), preferred_element_type=jnp.float32)
+            )
+            value_parts.append(
+                jnp.dot(
+                    probs.astype(jnp.bfloat16),
+                    columns(upper, head),
+                    preferred_element_type=jnp.float32,
+                )
+            )
+        both = jnp.concatenate(key_parts + value_parts, axis=1).astype(jnp.bfloat16)
+        return both, jnp.concatenate(query_parts, axis=0)
+
+    own_part, first = grads_of(own, own_mask)
+    mixed[...] = first
+
+    def backward_slot(index, carried):
+        @pl.when(live[index] == 1)
+        def _():
+            both, more = grads_of(others[index], key_segs[index] == query_segs)
+            parts[index % 2, index // 2] = both
+            mixed[...] += more
+
+        @pl.when(live[index] != 1)
+        def _():
+            parts[index % 2, index // 2] = jnp.zeros(own_ref.shape, jnp.bfloat16)
+
+        return carried
+
+    lax.fori_loop(0, slots, backward_slot, 0)
+    parts[core, 0] = own_part
+    q_grads[...] = (mixed[...] * scale.astype(jnp.float32)).T
 
 
 def call(kernel, number, operands, outs, spaces, out_spaces, scratch, remote, local):
@@ -398,7 +511,6 @@
     group_rows = model_count * tok_dev
     key_reach = min(SPAN * group_rows, group_rows * fsdp_count // 2)
     hops = (key_reach // group_rows + 1) // 2
-    score_scale = 1.0 / math.sqrt(head_dim)
     bf16, f32 = jnp.bfloat16, jnp.float32
     vmem, anywhere = pltpu.VMEM, pl.ANY
 
@@ -455,13 +567,13 @@
     group_index = fsdp_rank * group_rows + jnp.arange(group_rows, dtype=jnp.int32)
     group_seg, group_pos = token_segments(seq_lengths, group_index)
     group_cos, group_sin = rotary_tables(group_pos)
-    causal_mask = (
-        jnp.arange(group_rows, dtype=jnp.int32)[None, :]
-        <= jnp.arange(group_rows, dtype=jnp.int32)[:, None]
-    )
     projected = jnp.dot(h_attn, w_qkv, preferred_element_type=f32) + local_qkv_bias[None, :]
     projected = projected.reshape(group_rows, 3, local_heads, head_dim)
-    query_rows = rotate(projected[:, 0], group_cos, group_sin).astype(bf16)
+    query_rows = (
+        rotate(projected[:, 0], group_cos, group_sin)
+        .astype(bf16)
+        .reshape(group_rows, local_width)
+    )
     own_keys = rotate(projected[:, 1], group_cos, group_sin).astype(bf16)
     own_pair = jnp.concatenate(
         [own_keys.reshape(group_rows, local_width),
@@ -486,129 +598,44 @@
     hidden_low = hidden_grads.astype(bf16)
     mlp_input_part = contract_cols(hidden_low, w_up)
 
-    key_sets = [(own_pair, group_seg, True, None)]
-    for step in range(hops + 1):
-        for side in range(2):
-            source = (chip - step) * 2 + side
-            if step == 0:
-                if side == 1:
-                    continue
-                valid = core == 1
-            else:
-                valid = source >= 0
-            pair = others[step, side]
-            earlier = source * group_rows + jnp.arange(group_rows, dtype=jnp.int32)
-            earlier_seg, unused = token_segments(seq_lengths, earlier)
-            earlier_seg = jnp.where(valid, earlier_seg, -1)
-            key_sets.append((pair, earlier_seg, False, (step, side)))
-
-    def is_live(key_segs):
-        return key_segs[-1] == group_seg[0]
-
-    def block_scores(pair, key_segs, causal):
-        key_block = pair[:, :local_width].reshape(group_rows, local_heads, head_dim)
-        scores = (
-            jnp.einsum("qhd,khd->hqk", query_rows, key_block, preferred_element_type=f32)
-            * score_scale
-        )
-        key_mask = group_seg[:, None] == key_segs[None, :]
-        if causal:
-            key_mask = key_mask & causal_mask
-        return (scores, key_mask[None])
-
-    def stats_update(carried_state, pair, key_segs):
-        row_top, row_total = carried_state
-        scores, key_mask = block_scores(pair, key_segs, False)
-        masked = jnp.where(key_mask, scores, NEG_FILL)
-        new_top = jnp.maximum(row_top, jnp.max(masked, axis=-1))
-        new_total = row_total * jnp.exp(row_top - new_top) + jnp.sum(
-            jnp.where(key_mask, jnp.exp(masked - new_top[..., None]), 0.0), axis=-1
-        )
-        return (new_top, new_total)
-
-    scores, key_mask = block_scores(own_pair, group_seg, True)
-    masked = jnp.where(key_mask, scores, NEG_FILL)
-    row_top = jnp.max(masked, axis=-1)
-    row_total = jnp.sum(jnp.where(key_mask, jnp.exp(masked - row_top[..., None]), 0.0), axis=-1)
-    for pair, key_segs, causal, slot in key_sets[1:]:
-        row_top, row_total = lax.cond(
-            is_live(key_segs),
-            lambda carried_state: stats_update(carried_state, pair, key_segs),
-            lambda carried_state: carried_state,
-            (row_top, row_total),
-        )
-    row_lse = row_top + jnp.log(row_total)
-
-    def block_output(pair, key_segs, causal):
-        scores, key_mask = block_scores(pair, key_segs, causal)
-        attn_probs = jnp.where(key_mask, jnp.exp(scores - row_lse[..., None]), 0.0).astype(bf16)
-        value_block = pair[:, local_width:].reshape(group_rows, local_heads, head_dim)
-        return jnp.einsum("hqk,khd->qhd", attn_probs, value_block, preferred_element_type=f32)
-
-    zero_heads = jnp.zeros((group_rows, local_heads, head_dim), f32)
-    mixed = block_output(own_pair, group_seg, True)
-    for pair, key_segs, causal, slot in key_sets[1:]:
-        mixed = mixed + lax.cond(
-            is_live(key_segs), lambda: block_output(pair, key_segs, False), lambda: zero_heads
-        )
-    out_heads = mixed.astype(bf16)
-    out_flat = out_heads.reshape(group_rows, local_width)
+    slots = 2 * (hops + 1)
+    slot_step = jnp.arange(slots, dtype=jnp.int32) // 2
+    slot_source = (chip - slot_step) * 2 + jnp.arange(slots, dtype=jnp.int32) % 2
+    slot_tokens = (
+        slot_source[:, None] * group_rows + jnp.arange(group_rows, dtype=jnp.int32)[None, :]
+    )
+    slot_segs, unused = token_segments(seq_lengths, slot_tokens.reshape(-1))
+    slot_segs = slot_segs.reshape(slots, group_rows)
+    live = (
+        (slot_source >= 0) & (slot_source < fsdp_rank) & (slot_segs[:, -1] == group_seg[0])
+    ).astype(jnp.int32)
+    head_grads = jnp.dot(grad_rows, w_dense, preferred_element_type=f32).astype(bf16)
+    smem = pltpu.SMEM
+    stat = pltpu.VMEM((local_heads, 1, group_rows), f32)
+    out_flat, query_grads, part_stack = pl.pallas_call(
+        functools.partial(attention_kernel, local_heads, slots),
+        out_shape=[
+            jax.ShapeDtypeStruct((group_rows, local_width), bf16),
+            jax.ShapeDtypeStruct((group_rows, local_width), f32),
+            jax.ShapeDtypeStruct((2, hops + 1) + own_pair.shape, bf16),
+        ],
+        in_specs=[pl.BlockSpec(memory_space=smem)] + [pl.BlockSpec(memory_space=vmem)] * 7,
+        out_specs=[pl.BlockSpec(memory_space=vmem)] * 3,
+        scratch_shapes=[
+            stat, stat, pltpu.VMEM((local_width, group_rows), f32), stat, stat,
+        ],
+    )(
+        live,
+        query_rows,
+        own_pair,
+        others.reshape((slots,) + own_pair.shape),
+        head_grads,
+        group_seg[None, :],
+        group_seg[:, None],
+        slot_segs[:, :, None],
+    )
+    query_grads = query_grads.reshape(group_rows, local_heads, head_dim)
     branch_part = (mlp_part + contract_cols(out_flat, w_dense)).astype(bf16)
-    head_grads = (
-        jnp.dot(grad_rows, w_dense, preferred_element_type=f32)
-        .astype(bf16)
-        .reshape(group_rows, local_heads, head_dim)
-    )
-    row_delta = jnp.sum(head_grads.astype(f32) * out_heads.astype(f32), axis=-1).T
-
-    def block_grads(pair, key_segs, causal):
-        scores, key_mask = block_scores(pair, key_segs, causal)
-        attn_probs = jnp.where(key_mask, jnp.exp(scores - row_lse[..., None]), 0.0)
-        key_block = pair[:, :local_width].reshape(group_rows, local_heads, head_dim)
-        value_block = pair[:, local_width:].reshape(group_rows, local_heads, head_dim)
-        prob_grads = jnp.einsum(
-            "qhd,khd->hqk", head_grads, value_block, preferred_element_type=f32
-        )
-        score_grads = (attn_probs * (prob_grads - row_delta[..., None]) * score_scale).astype(bf16)
-        query_grads = jnp.einsum(
-            "hqk,khd->qhd", score_grads, key_block, preferred_element_type=f32
-        )
-        key_part = jnp.einsum(
-            "hqk,qhd->khd", score_grads, query_rows, preferred_element_type=f32
-        )
-        value_part = jnp.einsum(
-            "hqk,qhd->khd", attn_probs.astype(bf16), head_grads, preferred_element_type=f32
-        )
-        return (
-            query_grads,
-            jnp.concatenate(
-                [
-                    key_part.reshape(group_rows, local_width),
-                    value_part.reshape(group_rows, local_width),
-                ],
-                axis=1,
-            ).astype(bf16),
-        )
-
-    zero_pair = jnp.zeros((group_rows, 2 * local_width), bf16)
-    query_grads, own_part = block_grads(own_pair, group_seg, True)
-    parts = {}
-    for pair, key_segs, causal, slot in key_sets[1:]:
-        query_part, parts[slot] = lax.cond(
-            is_live(key_segs),
-            lambda: block_grads(pair, key_segs, False),
-            lambda: (zero_heads, zero_pair),
-        )
-        query_grads = query_grads + query_part
-    pair_part = parts[(0, 0)]
-    first = core == 0
-    near_parts = [jnp.where(first, own_part, pair_part), jnp.where(first, zero_pair, own_part)]
-    part_stack = jnp.stack(
-        [
-            jnp.stack([near_parts[side]] + [parts[(step, side)] for step in range(1, hops + 1)])
-            for side in range(2)
-        ]
-    )
     branch_stack = branch_part.reshape(model_count, tok_dev, model_width)
     block_shape = own_pair.shape
     pair_grads, branch_rows = call(

time: 345 us -> 215 us (0.62)
  Pallas kernels: 226 us -> 149 us
  local copies, waits for them, and re-layouts: 50.4 us -> 33.9 us
  matrix products: 38.8 us -> 23.2 us
  other arithmetic: 24.3 us -> 9.72 us
  between operations: 8.61 us -> 1.34 us
    pallas_call x5, Pallas kernels: 226 us -> 140 us  [call(): pl.pallas_call(kernel, out_shape=[jax.ShapeDtypeStruct(shape, dtype) for...]
    dot_general x6 -> x0, matrix products: 13.8 us -> none  [the longest x1 3.87 us: block_output(): jnp.einsum('hqk,khd->qhd', attn_probs, value_block, preferred_element_typ...]
    pallas_call x0 -> x1, Pallas kernels: none -> 8.41 us  [on_device(): pl.pallas_call(functools.partial(attention_kernel, local_heads, slots), o...]
    broadcast_in_dim x11 -> x1, local copies, waits for them, and re-layouts: 8.82 us -> 0.86 us  [token_segments(): segment_ids[:, None]]
    another operation x7 -> x3, other arithmetic: 7.15 us -> 0.24 us  [the longest x3 4.21 us: on_device(): jnp.stack([jnp.stack([near_parts[side]] + [parts[step, side] for step in...]
    slice x6 -> x1, local copies, waits for them, and re-layouts: 4.1 us -> 0.51 us  [on_device(): group_seg[0]]
where the time goes in v2:
time: 215 us; the launch traced here: 217 us
  Pallas kernels  149 us (69%)
  local copies, waits for them, and re-layouts  33.9 us (16%)
  matrix products  23.2 us (11%)
  other arithmetic  9.72 us (5%)
    pallas_call x5, Pallas kernels, call(): pl.pallas_call(kernel, out_shape=[jax.ShapeDtypeStruct(shape, dtype) for...  140 us
    dot_general x4, matrix products, contract_cols(): lax.dot_general(left, right, (((1,), (1,)), ((), ())), preferred_element_...  8.99 us
    pallas_call x1, Pallas kernels, on_device(): pl.pallas_call(functools.partial(attention_kernel, local_heads, slots), o...  8.41 us
    concatenate x1, local copies, waits for them, and re-layouts, on_device(): jnp.concatenate([contract_rows(h_attn, qkv_grads).astype(bf16), contract_...  5.81 us

profile of v2, /device:TPU:0, one launch (start us, length us, event | category | flops | bytes accessed | tf_op | source)
XLA Modules:
  0.0 217.1 jit_solution(11910823360396843612)
XLA Ops:
  0.7 1.0 copy-done
  1.9 1.0 dynamic-slice_bitcast_fusion
  2.9 1.9 concatenate.76.w_ref
  5.3 0.8 pad_maximum_fusion.2.t_ref
  6.2 0.6 convert_element_type.100.v_ref
  6.8 33.9 %shard_map.254 = (bf16[8,96,2304]{2,1,0:T(8,128)(2,1)}, f32[8,1,1248]{2,1,0:T(1,128)}, bf16[4,128,1536]{2,1,0:T(8,128)(2,1)}) custom-call(bf16[96,2304]{1,0:T(8,128)(2,1)} %concatenate.76.w_ref, f32[1,1248]{1,0:T(1,128)} %convert_element_type.100.v_ref, bf16[128,1536]{1,0:T(8,128)(2,1)} %pad_maximum_fusion.2.t_ref), custom_call_target="tpu_custom_call" | custom-call | tf_op jit(solution)/shard_map/pallas_call | solution.py:466
  40.8 0.7 slice_reduce_fusion
  41.7 0.9 add_reduce_fusion
  42.7 2.1 convolution_add_fusion.1
  44.9 0.5 copy-done.23
  46.4 0.9 pad_maximum_fusion.3.x_ref.own_ref
  47.3 18.2 %shard_map.255 = bf16[3,2,512,384]{3,2,1,0:T(8,128)(2,1)} custom-call(bf16[512,384]{1,0:T(8,128)(2,1)} %pad_maximum_fusion.3.x_ref.own_ref), custom_call_target="tpu_custom_call" | custom-call | tf_op jit(solution)/shard_map/pallas_call | solution.py:466
  65.6 0.8 copy.83.q_ref
  66.6 0.5 slice.164
  67.1 0.8 fusion.37
  68.0 0.5 and_convert_fusion.live
  68.5 2.5 %broadcast_in_dim_reshape.6.key_segs = s32[6,512,1]{2,1,0:T(8,128)} reshape(s32[3072]{0:T(1024)S(1)} %convert_reduce_fusion.4) | data formatting | bytes 24576 | tf_op jit(solution)/shard_map/broadcast_in_dim;reshape | solution.py:635
  71.0 1.6 convolution_convert_fusion.4
  72.7 0.8 copy.84.h_ref
  73.5 0.9 copy.85.own_seg
  74.4 8.4 %shard_map.256 = (bf16[512,192]{1,0:T(8,128)(2,1)}, f32[512,192]{1,0:T(8,128)}, bf16[2,3,512,384]{3,2,1,0:T(8,128)(2,1)}) custom-call(s32[6]{0:T(128)} %and_convert_fusion.live, bf16[512,192]{1,0:T(8,128)(2,1)} %copy.83.q_ref, bf16[512,384]{1,0:T(8,128)(2,1)} %pad_maximum_fusion.3.x_ref.own_ref, bf16[6,512,384]{2,1,0:T(8,128)(2,1)} %bitcast.60, ...), custom_call_target="tpu_custom_call" | custom-call | tf_op jit(solution)/shard_map/pallas_call | solution.py:615
  82.8 1.6 fusion.29
  84.4 0.7 slice.184
  85.3 3.6 %multiply_convert_fusion = (bf16[512,768]{1,0:T(8,128)(2,1)S(1)}, f32[512,768]{1,0:T(8,128)}) fusion(f32[768]{0:T(1024)S(1)} %dynamic_slice.15, bf16[768,2304]{1,0:T(8,128)(2,1)} %bitcast.81, f32[768]{0:T(1024)S(1)} %add.186, f32[768]{0:T(1024)S(1)} %mul.282, bf16[512,1536]{1,0:T(8,128)(2,1)} %bitcast.98), kind=kOutput, calls=%fused_computation.22 | convolution fusion | flops 607911936 | bytes 4334592 | tf_op jit(solution)/shard_map/dot_general | solution.py:594
  88.9 3.3 %add_convert_fusion.1 = bf16[512,768]{1,0:T(8,128)(2,1)} fusion(f32[512,768]{1,0:T(8,128)S(1)} %fusion.29, bf16[512,768]{1,0:T(8,128)(2,1)S(1)} %get-tuple-element.79, bf16[768,2304]{1,0:T(8,128)(2,1)} %bitcast.82), kind=kOutput, calls=%fused_computation.21 | convolution fusion | flops 604766208 | bytes 4325376 | tf_op jit(solution)/shard_map/dot_general | solution.py:97
  92.2 39.2 %shard_map.257 = (f32[512,384]{1,0:T(8,128)}, bf16[4,128,768]{2,1,0:T(8,128)(2,1)}) custom-call(bf16[2,3,512,384]{3,2,1,0:T(8,128)(2,1)} %get-tuple-element.30.p_ref, bf16[4,128,768]{2,1,0:T(8,128)(2,1)} %bitcast.75), custom_call_target="tpu_custom_call" | custom-call | tf_op jit(solution)/shard_map/pallas_call | solution.py:466
  131.3 1.1 slice.191
  133.3 1.2 slice.333
  134.5 2.2 %fusion.16 = f32[512,768]{1,0:T(8,128)S(1)} fusion(bf16[768,2304]{1,0:T(8,128)(2,1)} %bitcast.83, bf16[512,192]{1,0:T(8,128)(2,1)S(1)} %slice.333, bf16[512,192]{1,0:T(8,128)(2,1)S(1)} %copy.90, bf16[512,192]{1,0:T(8,128)(2,1)S(1)} %copy.89), kind=kOutput, calls=%fused_computation.37 | convolution fusion | flops 454754304 | bytes 3145728 | tf_op jit(solution)/shard_map/dot_general | solution.py:97
  136.8 2.8 %fusion.44 = (f32[768]{0:T(1024)S(1)}, bf16[512,768]{1,0:T(8,128)(2,1)S(1)}) fusion(f32[512,768]{1,0:T(8,128)} %get-tuple-element.80, bf16[768,2304]{1,0:T(8,128)(2,1)S(1)} %bitcast.84, bf16[512,1536]{1,0:T(8,128)(2,1)} %bitcast.99), kind=kOutput, calls=%fused_computation.130 | convolution fusion | flops 608304384 | bytes 4328448 | tf_op jit(solution)/shard_map/dot_general | solution.py:597
  139.6 1.9 fusion.41
  143.0 0.8 concatenate.101.v_ref
  143.8 2.1 convolution_convert_fusion.2
  146.3 0.8 convolution_convert_fusion.1
  147.4 0.8 convolution_convert_fusion
  148.2 2.1 pad_maximum_fusion
  150.3 5.8 %copy.91 = bf16[768,2304]{1,0:T(8,128)(2,1)} copy(bf16[768,2304]{0,1:T(8,128)(2,1)} %pad_maximum_fusion) | data formatting | bytes 7077888 | tf_op jit(solution)/shard_map/concatenate | solution.py:675
  156.1 33.6 %shard_map.258 = (f32[96,2304]{1,0:T(8,128)}, f32[1,1152]{1,0:T(1,128)}, bf16[4,128,768]{2,1,0:T(8,128)(2,1)}) custom-call(bf16[4,2,96,2304]{3,2,1,0:T(8,128)(2,1)} %bitcast.59, f32[4,2,1,1152]{3,2,1,0:T(1,128)} %concatenate.101.v_ref, bf16[4,128,768]{2,1,0:T(8,128)(2,1)} %bitcast.69), custom_call_target="tpu_custom_call" | custom-call | tf_op jit(solution)/shard_map/pallas_call | solution.py:466
  189.7 1.6 slice.335.g_ref
  191.4 15.6 %shard_map.259 = (bf16[4,96,768]{2,1,0:T(8,128)(2,1)}, f32[4,1,1152]{2,1,0:T(1,128)}) custom-call(bf16[96,768]{1,0:T(8,128)(2,1)} %slice.335.g_ref, f32[1,1152]{1,0:T(1,128)} %get-tuple-element.37.v_ref), custom_call_target="tpu_custom_call" | custom-call | tf_op jit(solution)/shard_map/pallas_call | solution.py:466
  206.9 1.1 slice.239
  208.5 1.1 copy.93
  210.3 1.0 reshape.411
  211.3 0.6 slice_bitcast_fusion.3
  211.9 0.6 slice_reduce_fusion.5
  212.5 0.6 slice_reduce_fusion.6
  213.7 0.9 multiply_add_fusion
  214.6 1.9 fusion.42
  (125 shorter events, 7.7 us)
Async XLA Ops:
  0.6 1.1 copy-start
  0.7 4.1 %copy-start.1 = (f32[128,768]{1,0:T(8,128)S(1)}, f32[128,768]{1,0:T(8,128)}, u32[]{:S(2)}) copy-start(f32[128,768]{1,0:T(8,128)} %param.15) | copy-start | bytes 1179652
  0.7 4.4 %copy-start.3 = (f32[128,768]{1,0:T(8,128)S(1)}, f32[128,768]{1,0:T(8,128)}, u32[]{:S(2)}) copy-start(f32[128,768]{1,0:T(8,128)} %param.16) | copy-start | bytes 1179652
  4.7 1.3 copy-start.11
  4.7 1.3 copy-start.12
  4.7 1.3 copy-start.13
  4.7 1.3 copy-start.14
  4.7 1.3 copy-start.15
  4.8 1.3 copy-start.16
  4.8 1.3 copy-start.17
  4.8 1.3 copy-start.18
  44.8 0.7 copy-start.23
  45.8 27.7 %copy-start.9 = (s32[512]{0:T(512)}, s32[512]{0:T(512)S(1)}, u32[]{:S(2)}) copy-start(s32[512]{0:T(512)S(1)} %convert_reduce_fusion.5) | copy-start | bytes 6148
  65.5 5.5 %copy-start.20 = (bf16[4,128,1536]{2,1,0:T(8,128)(2,1)S(1)}, bf16[4,128,1536]{2,1,0:T(8,128)(2,1)}, u32[]{:S(2)}) copy-start(bf16[4,128,1536]{2,1,0:T(8,128)(2,1)} %get-tuple-element.27) | copy-start | bytes 4718596
  88.9 3.3 %copy-start.24 = (bf16[512,768]{1,0:T(8,128)(2,1)}, bf16[512,768]{1,0:T(8,128)(2,1)S(1)}, u32[]{:S(2)}) copy-start(bf16[512,768]{1,0:T(8,128)(2,1)S(1)} %get-tuple-element.79) | copy-start | bytes 2359300
  131.3 1.3 copy-start.6
  134.5 2.3 %copy-start.8 = (bf16[8,96,2304]{2,1,0:T(8,128)(2,1)S(1)}, bf16[8,96,2304]{2,1,0:T(8,128)(2,1)}, u32[]{:S(2)}) copy-start(bf16[8,96,2304]{2,1,0:T(8,128)(2,1)} %get-tuple-element.29) | copy-start | bytes 10616836
  136.8 2.8 %copy-start.21 = (bf16[4,128,1536]{2,1,0:T(8,128)(2,1)S(1)}, bf16[4,128,1536]{2,1,0:T(8,128)(2,1)}, u32[]{:S(2)}) copy-start(bf16[4,128,1536]{2,1,0:T(8,128)(2,1)} %get-tuple-element.27) | copy-start | bytes 4718596
  143.8 2.1 copy-start.7
  143.8 2.1 copy-start.22
  146.3 1.1 copy-start.25
  208.4 1.3 copy-start.2
  209.8 1.4 copy-start.10
  209.8 3.3 %copy-start.5 = (bf16[4,128,768]{2,1,0:T(8,128)(2,1)S(1)}, bf16[4,128,768]{2,1,0:T(8,128)(2,1)}, u32[]{:S(2)}) copy-start(bf16[4,128,768]{2,1,0:T(8,128)(2,1)} %get-tuple-element.35) | copy-start | bytes 2359300
  210.0 3.5 %copy-start.4 = (bf16[4,128,768]{2,1,0:T(8,128)(2,1)S(1)}, bf16[4,128,768]{2,1,0:T(8,128)(2,1)}, u32[]{:S(2)}) copy-start(bf16[4,128,768]{2,1,0:T(8,128)(2,1)} %get-tuple-element.32) | copy-start | bytes 2359300
  211.9 4.7 %copy-start.19 = (f32[96]{0:T(128)}, f32[96]{0:T(128)S(1)}, u32[]{:S(2)}) copy-start(f32[96]{0:T(128)S(1)} %get-tuple-element.113) | copy-start | bytes 1156

commit v3 on v2

--- a/solution.py
+++ b/solution.py
@@ -187,23 +187,30 @@
     return waits
 
 
-def open_kernel(chip_count, model_count, w_ref, v_ref, t_ref, w_out, v_out, t_out, s, r, l):
+def open_kernel(chip_count, model_count, count, *refs):
+    sources, t_ref = refs[:count], refs[count]
+    targets, t_out = refs[count + 1 : 2 * count + 1], refs[2 * count + 1]
+    enter(chip_count, model_count)
+    copies = Copies(*refs[2 * count + 2 :])
+    waits = model_exchange(copies, t_ref, t_out, model_count, True)
+    sent = []
+    for source, target in zip(sources, targets):
+        near, far = gather_start(copies, source, target, chip_count)
+        waits += near
+        sent.append(far)
+    for target, far in zip(targets, sent):
+        waits += gather_forward(copies, target, far, chip_count)
+    for far in sent:
+        for copy in far:
+            copy.wait_send()
+    for copy in waits:
+        copy.wait()
+
+
+def keys_kernel(chip_count, model_count, hops, x_ref, t_ref, out, t_out, s, r, l):
     enter(chip_count, model_count)
     copies = Copies(s, r, l)
     tokens = model_exchange(copies, t_ref, t_out, model_count, True)
-    near_v, far_v = gather_start(copies, v_ref, v_out, chip_count)
-    near_w, far_w = gather_start(copies, w_ref, w_out, chip_count)
-    more = gather_forward(copies, v_out, far_v, chip_count)
-    more += gather_forward(copies, w_out, far_w, chip_count)
-    for copy in far_v + far_w:
-        copy.wait_send()
-    for copy in tokens + near_v + near_w + more:
-        copy.wait()
-
-
-def keys_kernel(chip_count, hops, x_ref, out, s, r, l):
-    enter(chip_count, 1)
-    copies = Copies(s, r, l)
     chip, core, model = place()
     pair = (chip * 2 + (1 - core), model)
     near = copies.remote(x_ref, out.at[0, core], pair)
@@ -226,6 +233,8 @@
             copy.start()
 
     near.wait()
+    for copy in tokens:
+        copy.wait()
     for step in range(1, hops + 1):
 
         @pl.when(chip >= step)
@@ -323,29 +332,36 @@
         copy.wait_send()
 
 
-def close_kernel(
-    chip_count, model_count, g_ref, v_ref, b_ref, g_out, v_out, b_out,
-    g_near, g_sums, g_far, v_near, v_sums, v_far, s, r, l,
-):
+def close_kernel(chip_count, model_count, count, *refs):
+    sources, b_ref = refs[:count], refs[count]
+    targets, b_out = refs[count + 1 : 2 * count + 1], refs[2 * count + 1]
+    room = refs[2 * count + 2 : 5 * count + 2]
     enter(chip_count, model_count)
-    copies = Copies(s, r, l)
-    v_started = reduce_near(copies, v_ref, v_near, chip_count)
-    g_started = reduce_near(copies, g_ref, g_near, chip_count)
+    copies = Copies(*refs[5 * count + 2 :])
+    started = [
+        reduce_near(copies, source, room[3 * at], chip_count)
+        for at, source in enumerate(sources)
+    ]
     branch = model_exchange(copies, b_ref, b_out, model_count, False)
-    v_sent = reduce_far(copies, v_ref, v_near, v_sums, v_far, v_out, v_started, chip_count)
-    g_sent = reduce_far(copies, g_ref, g_near, g_sums, g_far, g_out, g_started, chip_count)
-    reduce_end(v_out, v_far, v_started, v_sent)
-    reduce_end(g_out, g_far, g_started, g_sent)
+    sent = [
+        reduce_far(
+            copies, source, *room[3 * at : 3 * at + 3], targets[at], started[at], chip_count
+        )
+        for at, source in enumerate(sources)
+    ]
+    for at, target in enumerate(targets):
+        reduce_end(target, room[3 * at + 2], started[at], sent[at])
     for copy in branch:
         copy.wait()
 
 
-def last_kernel(model_count, g_ref, v_ref, g_out, v_out, s, r, l):
+def last_kernel(model_count, count, *refs):
     enter(0, model_count)
-    copies = Copies(s, r, l)
-    started = model_exchange(copies, v_ref, v_out, model_count, True)
-    started += model_exchange(copies, g_ref, g_out, model_count, True)
-    for copy in started:
+    copies = Copies(*refs[2 * count :])
+    waits = []
+    for source, target in zip(refs[:count], refs[count : 2 * count]):
+        waits += model_exchange(copies, source, target, model_count, True)
+    for copy in waits:
         copy.wait()
 
 
@@ -516,35 +532,33 @@
 
     own_qkv = lax.dynamic_slice_in_dim(qkv_weight, model_rank * local_heads, local_heads, 2)
     own_dense = lax.dynamic_slice_in_dim(dense_weight, model_rank * local_width, local_width, 0)
-    pack = jnp.concatenate(
-        [own_qkv.reshape(owned, 3 * local_width), own_dense.T, up_weight, down_weight], axis=1
-    )
     vectors = (qkv_bias, dense_bias, up_bias, down_bias, gain_attn, beta_attn, gain_mlp, beta_mlp)
     vector_pack = jnp.concatenate(vectors).astype(f32)[None, :]
     normed, inv_std = norm_parts(layer_input)
     grad_low = cotangent.astype(bf16)
-    token_pack = jnp.concatenate([normed.astype(bf16), grad_low], axis=1)
-    columns = pack.shape[1]
-    weights, vector_all, token_rows = call(
-        functools.partial(open_kernel, chip_count, model_count),
+    normed_low = normed.astype(bf16)
+    owned_parts = (
+        vector_pack,
+        own_qkv.reshape(owned, 3 * local_width),
+        up_weight,
+        own_dense.T,
+        down_weight,
+    )
+    vector_all, w_qkv, w_up, w_dense, w_down, normed_rows = call(
+        functools.partial(open_kernel, chip_count, model_count, len(owned_parts)),
         0,
-        (pack, vector_pack, token_pack),
-        [
-            ((fsdp_count,) + pack.shape, bf16),
-            ((fsdp_count,) + vector_pack.shape, f32),
-            ((model_count,) + token_pack.shape, bf16),
-        ],
-        [anywhere] * 3,
-        [anywhere] * 3,
+        owned_parts + (normed_low,),
+        [((fsdp_count,) + part.shape, part.dtype) for part in owned_parts]
+        + [((model_count,) + normed_low.shape, bf16)],
+        [anywhere] * (len(owned_parts) + 1),
+        [anywhere] * (len(owned_parts) + 1),
         [],
-        (model_count - 1) + 2 * (2 * chip_count - 1),
-        3,
-    )
-    weights = weights.reshape(model_width, columns)
-    w_qkv = weights[:, : 3 * local_width]
-    w_dense = weights[:, 3 * local_width : 4 * local_width]
-    w_up = weights[:, 4 * local_width : 4 * local_width + hidden_local]
-    w_down = weights[:, 4 * local_width + hidden_local :]
+        (model_count - 1) + len(owned_parts) * (2 * chip_count - 1),
+        len(owned_parts) + 1,
+    )
+    w_qkv, w_up, w_dense, w_down = (
+        part.reshape(model_width, part.shape[2]) for part in (w_qkv, w_up, w_dense, w_down)
+    )
     full = []
     at = 0
     for vector in vectors:
@@ -558,9 +572,7 @@
     local_up_bias = lax.dynamic_slice_in_dim(
         full_up_bias, model_rank * hidden_local, hidden_local, 0
     )
-    token_rows = token_rows.reshape(group_rows, 2 * model_width)
-    normed_rows = token_rows[:, :model_width].astype(f32)
-    grad_rows = token_rows[:, model_width:]
+    normed_rows = normed_rows.reshape(group_rows, model_width).astype(f32)
     h_attn = (normed_rows * gain_one + shift_one).astype(bf16)
     h_mlp = (normed_rows * gain_two + shift_two).astype(bf16)
 
@@ -579,17 +591,18 @@
         [own_keys.reshape(group_rows, local_width),
          projected[:, 2].astype(bf16).reshape(group_rows, local_width)], axis=1
     )
-    (others,) = call(
-        functools.partial(keys_kernel, chip_count, hops),
+    others, grad_rows = call(
+        functools.partial(keys_kernel, chip_count, model_count, hops),
         1,
-        (own_pair,),
-        [((hops + 1, 2) + own_pair.shape, bf16)],
-        [anywhere],
-        [anywhere],
+        (own_pair, grad_low),
+        [((hops + 1, 2) + own_pair.shape, bf16), ((model_count,) + grad_low.shape, bf16)],
+        [anywhere] * 2,
+        [anywhere] * 2,
         [],
-        1 + 2 * hops,
-        0,
-    )
+        1 + 2 * hops + model_count - 1,
+        1,
+    )
+    grad_rows = grad_rows.reshape(group_rows, model_width)
 
     pre_act = jnp.dot(h_mlp, w_up, preferred_element_type=f32) + local_up_bias[None, :]
     activation = gelu_value(pre_act).astype(bf16)
@@ -672,15 +685,15 @@
         ],
         axis=1,
     ).astype(bf16)
-    grad_parts = jnp.concatenate(
-        [
-            contract_rows(h_attn, qkv_grads).astype(bf16),
-            contract_rows(grad_rows, out_flat).astype(bf16),
-            contract_rows(h_mlp, hidden_low).astype(bf16),
-            contract_rows(grad_rows, activation).astype(bf16),
-        ],
-        axis=1,
-    ).reshape(chip_count, 2, owned, columns)
+    grad_parts = tuple(
+        part.astype(bf16).reshape(chip_count, 2, owned, part.shape[1])
+        for part in (
+            contract_rows(h_mlp, hidden_low),
+            contract_rows(grad_rows, activation),
+            contract_rows(grad_rows, out_flat),
+            contract_rows(h_attn, qkv_grads),
+        )
+    )
     attn_input_part = contract_cols(qkv_grads, w_qkv)
     hat_part = (attn_input_part * gain_one + mlp_input_part * gain_two).astype(bf16)
     hat_stack = hat_part.reshape(model_count, tok_dev, model_width)
@@ -708,49 +721,43 @@
     small_pack = jnp.concatenate(small, axis=1)
     small_width = small_pack.shape[1]
     small_pack = small_pack.reshape(chip_count, 2, 1, small_width)
-    grad_shape, small_shape = (owned, columns), (1, small_width)
-    grads, small_sums, hat_rows = call(
-        functools.partial(close_kernel, chip_count, model_count),
+    summed = (small_pack,) + grad_parts
+    small_sums, grad_up_w, grad_down_w, dense_sums, qkv_sums, hat_rows = call(
+        functools.partial(close_kernel, chip_count, model_count, len(summed)),
         3,
-        (grad_parts, small_pack, hat_stack),
-        [(grad_shape, f32), (small_shape, f32), (hat_stack.shape, bf16)],
-        [vmem, vmem, anywhere],
-        [vmem, vmem, anywhere],
+        summed + (hat_stack,),
+        [(part.shape[2:], f32) for part in summed] + [(hat_stack.shape, bf16)],
+        [vmem] * len(summed) + [anywhere],
+        [vmem] * len(summed) + [anywhere],
         [
-            pltpu.VMEM((chip_count,) + grad_shape, bf16),
-            pltpu.VMEM((chip_count - 1,) + grad_shape, bf16),
-            pltpu.VMEM((chip_count - 1,) + grad_shape, bf16),
-            pltpu.VMEM((chip_count,) + small_shape, f32),
-            pltpu.VMEM((chip_count - 1,) + small_shape, f32),
-            pltpu.VMEM((chip_count - 1,) + small_shape, f32),
+            pltpu.VMEM((slots_of,) + part.shape[2:], part.dtype)
+            for part in summed
+            for slots_of in (chip_count, chip_count - 1, chip_count - 1)
         ],
-        2 * (2 * chip_count - 1) + model_count - 1,
+        len(summed) * (2 * chip_count - 1) + model_count - 1,
         1,
     )
-    heavy = grads[:, : 4 * local_width].astype(bf16)
-    heavy_all, small_all = call(
-        functools.partial(last_kernel, model_count),
+    shared = (small_sums, dense_sums.astype(bf16), qkv_sums.astype(bf16))
+    small_all, dense_all, qkv_all = call(
+        functools.partial(last_kernel, model_count, len(shared)),
         4,
-        (heavy, small_sums),
-        [((model_count,) + heavy.shape, bf16), ((model_count,) + small_shape, f32)],
-        [anywhere] * 2,
-        [anywhere] * 2,
+        shared,
+        [((model_count,) + part.shape, part.dtype) for part in shared],
+        [anywhere] * len(shared),
+        [anywhere] * len(shared),
         [],
-        2 * (model_count - 1),
-        2,
+        len(shared) * (model_count - 1),
+        len(shared),
     )
     grad_hat = jnp.sum(hat_rows.astype(f32), axis=0)
     input_grad = cotangent + norm_back(grad_hat, normed, inv_std)
-    heavy_all = heavy_all.astype(f32)
     grad_qkv_w = (
-        heavy_all[:, :, : 3 * local_width]
+        qkv_all.astype(f32)
         .reshape(model_count, owned, 3, local_heads, head_dim)
         .transpose(1, 2, 0, 3, 4)
         .reshape(owned, 3, head_count, head_dim)
     )
-    grad_dense_w = (
-        heavy_all[:, :, 3 * local_width :].transpose(0, 2, 1).reshape(model_width, owned)
-    )
+    grad_dense_w = dense_all.astype(f32).transpose(0, 2, 1).reshape(model_width, owned)
     small_total = jnp.sum(small_all, axis=0)[0]
     final = []
     at = 0
@@ -768,9 +775,9 @@
         final[4],
         final[5],
         final[6],
-        grads[:, 4 * local_width : 4 * local_width + hidden_local],
+        grad_up_w,
         final[2],
-        grads[:, 4 * local_width + hidden_local :],
+        grad_down_w,
         final[1],
     )
 

time: 215 us -> 216 us (level); the launches traced: 217 us -> 215 us
  other arithmetic: 9.72 us -> 16.9 us
  Pallas kernels: 149 us -> 142 us
  local copies, waits for them, and re-layouts: 33.9 us -> 28.2 us
  matrix products: 23.2 us -> 27.3 us
    concatenate x2 -> x0, local copies, waits for them, and re-layouts: 7.66 us -> none  [the longest x1 5.81 us: on_device(): jnp.concatenate([contract_rows(h_attn, qkv_grads).astype(bf16), contract_...]
    pallas_call x5, Pallas kernels: 140 us -> 133 us  [call(): pl.pallas_call(kernel, out_shape=[jax.ShapeDtypeStruct(shape, dtype) for...]
    slice x4 -> x0, local copies, waits for them, and re-layouts: 5.03 us -> none  [the longest x1 1.9 us: on_device(): grads[:, 4 * local_width + hidden_local:]]
    convert_element_type x1 -> x4, other arithmetic: 0.09 us -> 4.44 us  [the longest x1 2.36 us: on_device(): h_mlp = (normed_rows * gain_two + shift_two).astype(bf16)]
    dot_general x4, matrix products: 4.1 us -> 8.29 us  [contract_rows(): lax.dot_general(left, right, (((0,), (0,)), ((), ())), preferred_element_...]
    convert_element_type x0 -> x2, local copies, waits for them, and re-layouts: none -> 3.13 us  [on_device(): part.astype(bf16).reshape(chip_count, 2, owned, part.shape[1])]
    concatenate x2 -> x0, other arithmetic: 2.85 us -> none  [the longest x1 2.07 us: on_device(): jnp.concatenate([contract_rows(h_attn, qkv_grads).astype(bf16), contract_...]
    reshape x1 -> x4, local copies, waits for them, and re-layouts: 0.97 us -> 3.58 us  [the longest x2 2.35 us: on_device(): grad_qkv_w = qkv_all.astype(f32).reshape(model_count, owned, 3, local_hea...]
where the time goes in v3:
time: 216 us; the launch traced here: 215 us
  Pallas kernels  142 us (66%)
  local copies, waits for them, and re-layouts  28.2 us (13%)
  matrix products  27.3 us (13%)
  other arithmetic  16.9 us (8%)
    pallas_call x5, Pallas kernels, call(): pl.pallas_call(kernel, out_shape=[jax.ShapeDtypeStruct(shape, dtype) for...  133 us
    pallas_call x1, Pallas kernels, on_device(): pl.pallas_call(functools.partial(attention_kernel, local_heads, slots), o...  8.4 us
    dot_general x4, matrix products, contract_rows(): lax.dot_general(left, right, (((0,), (0,)), ((), ())), preferred_element_...  8.29 us
    dot_general x4, matrix products, contract_cols(): lax.dot_general(left, right, (((1,), (1,)), ((), ())), preferred_element_...  8.23 us

profile of v3, /device:TPU:0, one launch (start us, length us, event | category | flops | bytes accessed | tf_op | source)
XLA Modules:
  0.0 215.5 jit_solution(16750782242117128883)
XLA Ops:
  0.8 0.9 reduce-window.8
  2.4 0.8 fusion.19
  3.8 0.7 concatenate.67
  4.4 0.7 concatenate.69
  5.1 0.8 concatenate.75
  6.6 0.8 copy.84.refs_1_
  7.4 1.6 dynamic-slice_bitcast_fusion.refs_3_
  8.9 1.1 reduce_sum.157
  10.1 1.2 multiply_reduce_fusion.1
  11.3 0.8 fusion.18.refs_5_
  12.1 29.8 %shard_map.254 = (f32[8,1,1248]{2,1,0:T(1,128)}, bf16[8,96,576]{2,1,0:T(8,128)(2,1)}, bf16[8,96,768]{2,1,0:T(8,128)(2,1)}, bf16[8,96,192]{2,1,0:T(8,128)(2,1)}, ...) custom-call(f32[1,1248]{1,0:T(1,128)} %convert_element_type.121.refs_0_, bf16[96,576]{1,0:T(8,128)(2,1)} %copy.84.refs_1_, ...), custom_call_target="tpu_custom_call" | custom-call | tf_op jit(solution)/shard_map/pallas_call | solution.py:482
  41.9 1.5 add_reduce_fusion
  43.7 2.4 %fusion.8 = (bf16[4,128,768]{2,1,0:T(8,128)(2,1)}, bf16[4,128,768]{2,1,0:T(8,128)(2,1)S(1)}) fusion(bf16[4,128,768]{2,1,0:T(8,128)(2,1)} %get-tuple-element.36, f32[768]{0:T(1024)S(1)} %add.196, f32[768]{0:T(1024)S(1)} %mul.292, f32[768]{0:T(1024)S(1)} %add.188, f32[768]{0:T(1024)S(1)} %mul.275), kind=kLoop, calls=%fused_computation.17 | loop fusion | flops 2752512 | bytes 2371584 | tf_op jit(solution)/shard_map/convert_element_type | solution.py:577
  46.3 1.9 convolution_add_fusion.1
  49.2 0.8 copy.87.q_ref
  50.4 0.9 pad_maximum_fusion.1.x_ref.own_ref
  51.3 1.3 fusion.26
  52.6 19.3 %shard_map.255 = (bf16[3,2,512,384]{3,2,1,0:T(8,128)(2,1)}, bf16[4,128,768]{2,1,0:T(8,128)(2,1)}) custom-call(bf16[512,384]{1,0:T(8,128)(2,1)} %pad_maximum_fusion.1.x_ref.own_ref, bf16[128,768]{1,0:T(8,128)(2,1)} %get-tuple-element.89.t_ref), custom_call_target="tpu_custom_call" | custom-call | tf_op jit(solution)/shard_map/pallas_call | solution.py:482
  71.9 1.6 convolution_convert_fusion.4
  73.5 0.8 copy.88.h_ref
  74.3 0.9 copy.89.own_seg
  75.2 2.6 %broadcast_in_dim_reshape.6.key_segs = s32[6,512,1]{2,1,0:T(8,128)} reshape(s32[3072]{0:T(1024)S(1)} %convert_reduce_fusion.4) | data formatting | bytes 24576 | tf_op jit(solution)/shard_map/broadcast_in_dim;reshape | solution.py:648
  77.8 8.4 %shard_map.256 = (bf16[512,192]{1,0:T(8,128)(2,1)}, f32[512,192]{1,0:T(8,128)}, bf16[2,3,512,384]{3,2,1,0:T(8,128)(2,1)}) custom-call(s32[6]{0:T(128)} %and_convert_fusion.live, bf16[512,192]{1,0:T(8,128)(2,1)} %copy.87.q_ref, bf16[512,384]{1,0:T(8,128)(2,1)} %pad_maximum_fusion.1.x_ref.own_ref, bf16[6,512,384]{2,1,0:T(8,128)(2,1)} %bitcast.106, ...), custom_call_target="tpu_custom_call" | custom-call | tf_op jit(solution)/shard_map/pallas_call | solution.py:628
  86.2 1.4 fusion.28
  87.7 3.6 %multiply_convert_fusion = (bf16[512,768]{1,0:T(8,128)(2,1)S(1)}, f32[512,768]{1,0:T(8,128)}) fusion(f32[768]{0:T(1024)S(1)} %dynamic_slice.15, bf16[512,768]{1,0:T(8,128)(2,1)} %bitcast.124, bf16[768,768]{1,0:T(8,128)(2,1)} %bitcast.141), kind=kOutput, calls=%fused_computation.27 | convolution fusion | flops 606339072 | bytes 4328448 | tf_op jit(solution)/shard_map/dot_general | solution.py:607
  91.3 1.7 add_convert_fusion.1
  93.0 29.3 %shard_map.257 = (f32[512,384]{1,0:T(8,128)}, bf16[4,128,768]{2,1,0:T(8,128)(2,1)}) custom-call(bf16[2,3,512,384]{3,2,1,0:T(8,128)(2,1)} %get-tuple-element.42.p_ref, bf16[4,128,768]{2,1,0:T(8,128)(2,1)} %bitcast.126), custom_call_target="tpu_custom_call" | custom-call | tf_op jit(solution)/shard_map/pallas_call | solution.py:482
  122.3 1.2 slice.235
  123.5 1.1 slice.151
  124.8 1.2 copy.91
  127.3 3.8 %fusion.27 = (f32[768]{0:T(1024)S(1)}, bf16[512,768]{1,0:T(8,128)(2,1)}) fusion(f32[512,768]{1,0:T(8,128)} %get-tuple-element.102, bf16[512,768]{1,0:T(8,128)(2,1)S(1)} %bitcast.103, bf16[768,768]{1,0:T(8,128)(2,1)} %bitcast.143), kind=kOutput, calls=%fused_computation.116 | convolution fusion | flops 608304384 | bytes 4328448 | tf_op jit(solution)/shard_map/dot_general | solution.py:610
  131.3 2.4 %fusion.16 = f32[512,768]{1,0:T(8,128)S(1)} fusion(bf16[768,768]{1,0:T(8,128)(2,1)} %bitcast.142, bf16[512,768]{1,0:T(8,128)(2,1)} %get-tuple-element.104), kind=kOutput, calls=%fused_computation.47 | convolution fusion | flops 603979776 | bytes 3538944 | tf_op jit(solution)/shard_map/dot_general | solution.py:97
  133.8 2.7 %fusion.25 = (f32[768]{0:T(1024)S(1)}, f32[768]{0:T(1024)S(1)}, bf16[512,768]{1,0:T(8,128)(2,1)}, f32[768]{0:T(1024)S(1)}, f32[768]{0:T(1024)S(1)}, /*index=5*/bf16[512,768]{1,0:T(8,128)(2,1)}, bf16[512,768]{1,0:T(8,128)(2,1)}) fusion(bf16[4,128,768]{2,1,0:T(8,128)(2,1)S(1)} %copy-done.7, f32[512,768]{1,0:T(8,128)S(1)} %fusion.16, f32[768]{0:T(1024)S(1)} %copy-done.19, ...), kind=kOutput, calls=%fused_computation.114 | convolution fusion | flops 461435904 | bytes 6217728 | tf_op jit(solution)/shard_map/dot_general | solution.py:97
  136.9 0.8 concatenate.89.refs_0_
  137.6 3.3 %convolution_convert_fusion.1 = bf16[768,768]{1,0:T(8,128)(2,1)} fusion(bf16[512,768]{1,0:T(8,128)(2,1)} %get-tuple-element.75, bf16[512,768]{1,0:T(8,128)(2,1)} %get-tuple-element.104), kind=kOutput, calls=%fused_computation.30 | convolution fusion | flops 604569600 | bytes 2752512 | tf_op jit(solution)/shard_map/dot_general | solution.py:91
  140.9 1.8 convolution_convert_fusion
  143.1 0.9 copy.95
  144.0 2.8 %convolution_convert_fusion.2 = bf16[768,576]{0,1:T(8,128)(2,1)} fusion(bf16[512,768]{1,0:T(8,128)(2,1)} %get-tuple-element.74, bf16[512,192]{1,0:T(8,128)(2,1)S(1)} %slice.235, bf16[512,192]{1,0:T(8,128)(2,1)S(1)} %copy.94, bf16[512,192]{1,0:T(8,128)(2,1)S(1)} %copy.93), kind=kOutput, calls=%fused_computation.32 | convolution fusion | flops 455196672 | bytes 2260992 | tf_op jit(solution)/shard_map/dot_general | solution.py:91
  146.8 2.2 %copy.96 = bf16[768,576]{1,0:T(8,128)(2,1)} copy(bf16[768,576]{0,1:T(8,128)(2,1)} %convolution_convert_fusion.2) | data formatting | bytes 1769472 | tf_op jit(solution)/shard_map/convert_element_type | solution.py:689
  149.1 37.3 %shard_map.258 = (f32[1,1152]{1,0:T(1,128)}, f32[96,768]{1,0:T(8,128)}, f32[96,768]{1,0:T(8,128)}, f32[96,192]{1,0:T(8,128)}, f32[96,576]{1,0:T(8,128)}, /*index=5*/bf16[4,128,768]{2,1,0:T(8,128)(2,1)}) custom-call(f32[4,2,1,1152]{3,2,1,0:T(1,128)} %concatenate.89.refs_0_, bf16[4,2,96,768]{3,2,1,0:T(8,128)(2,1)} %bitcast.111, ...), custom_call_target="tpu_custom_call" | custom-call | tf_op jit(solution)/shard_map/pallas_call | solution.py:482
  186.4 1.5 convert_reduce_fusion
  188.3 0.9 multiply_add_fusion
  190.5 17.5 %shard_map.259 = (f32[4,1,1152]{2,1,0:T(1,128)}, bf16[4,96,192]{2,1,0:T(8,128)(2,1)}, bf16[4,96,576]{2,1,0:T(8,128)(2,1)}) custom-call(f32[1,1152]{1,0:T(1,128)} %get-tuple-element.50.refs_0_, bf16[96,192]{1,0:T(8,128)(2,1)} %convert_element_type.149.refs_1_, bf16[96,576]{1,0:T(8,128)(2,1)} %convert_element_type.150.refs_2_), custom_call_target="tpu_custom_call" | custom-call | tf_op jit(solution)/shard_map/pallas_call | solution.py:482
  208.1 1.3 copy.97
  209.3 1.1 copy.98
  211.4 1.0 reshape.474
  214.0 0.7 copy.106
  214.8 0.7 copy.107
  (144 shorter events, 10.4 us)
Async XLA Ops:
  0.6 5.9 %copy-start = (bf16[96,3,12,64]{0,3,2,1:T(8,128)(2,1)S(1)}, bf16[96,3,12,64]{0,3,2,1:T(8,128)(2,1)}, u32[]{:S(2)}) copy-start(bf16[96,3,12,64]{0,3,2,1:T(8,128)(2,1)} %param.22) | copy-start | bytes 1327108
  0.7 10.6 %copy-start.1 = (f32[128,768]{1,0:T(8,128)S(1)}, f32[128,768]{1,0:T(8,128)}, u32[]{:S(2)}) copy-start(f32[128,768]{1,0:T(8,128)} %param.15) | copy-start | bytes 1179652
  1.9 72.5 %copy-start.14 = (s32[512]{0:T(512)}, s32[512]{0:T(512)S(1)}, u32[]{:S(2)}) copy-start(s32[512]{0:T(512)S(1)} %convert_reduce_fusion.5) | copy-start | bytes 6148
  10.1 36.0 %copy-start.26 = (f32[128]{0:T(128)}, f32[128]{0:T(128)S(1)}, u32[]{:S(2)}) copy-start(f32[128]{0:T(128)S(1)} %broadcast_multiply_fusion.2) | copy-start | bytes 1540
  11.3 34.8 %copy-start.28 = (f32[128]{0:T(128)}, f32[128]{0:T(128)S(1)}, u32[]{:S(2)}) copy-start(f32[128]{0:T(128)S(1)} %add_rsqrt_fusion) | copy-start | bytes 1540
  41.9 4.2 %copy-start.13 = (f32[8,1,1248]{2,1,0:T(1,128)S(1)}, f32[8,1,1248]{2,1,0:T(1,128)}, u32[]{:S(2)}) copy-start(f32[8,1,1248]{2,1,0:T(1,128)} %get-tuple-element.37) | copy-start | bytes 119812
  43.5 4.7 %copy-start.16 = (f32[768]{0:T(1024)}, f32[768]{0:T(1024)S(1)}, u32[]{:S(2)}) copy-start(f32[768]{0:T(1024)S(1)} %add.196) | copy-start | bytes 9220
  43.6 4.6 %copy-start.18 = (f32[768]{0:T(1024)}, f32[768]{0:T(1024)S(1)}, u32[]{:S(2)}) copy-start(f32[768]{0:T(1024)S(1)} %mul.292) | copy-start | bytes 9220
  43.7 4.6 %copy-start.20 = (f32[768]{0:T(1024)}, f32[768]{0:T(1024)S(1)}, u32[]{:S(2)}) copy-start(f32[768]{0:T(1024)S(1)} %add.188) | copy-start | bytes 9220
  43.7 4.5 %copy-start.22 = (f32[768]{0:T(1024)}, f32[768]{0:T(1024)S(1)}, u32[]{:S(2)}) copy-start(f32[768]{0:T(1024)S(1)} %mul.275) | copy-start | bytes 9220
  48.2 0.7 copy-start.33
  49.2 2.1 copy-start.3
  50.1 21.8 %copy-start.4 = (bf16[8,96,192]{2,1,0:T(8,128)(2,1)S(1)}, bf16[8,96,192]{2,1,0:T(8,128)(2,1)}, u32[]{:S(2)}) copy-start(bf16[8,96,192]{2,1,0:T(8,128)(2,1)} %get-tuple-element.41) | copy-start | bytes 884740
  87.7 3.6 %copy-start.31 = (bf16[8,96,768]{2,1,0:T(8,128)(2,1)S(1)}, bf16[8,96,768]{2,1,0:T(8,128)(2,1)}, u32[]{:S(2)}) copy-start(bf16[8,96,768]{2,1,0:T(8,128)(2,1)} %get-tuple-element.44) | copy-start | bytes 3538948
  91.3 1.7 copy-start.34
  126.1 1.3 copy-start.2
  126.1 1.1 copy-start.24
  131.3 2.5 %copy-start.7 = (bf16[4,128,768]{2,1,0:T(8,128)(2,1)S(1)}, bf16[4,128,768]{2,1,0:T(8,128)(2,1)}, u32[]{:S(2)}) copy-start(bf16[4,128,768]{2,1,0:T(8,128)(2,1)} %get-tuple-element.36) | copy-start | bytes 2359300
  131.3 2.5 %copy-start.17 = (f32[768]{0:T(1024)S(1)}, f32[768]{0:T(1024)}, u32[]{:S(2)}) copy-start(f32[768]{0:T(1024)} %copy-done.16) | copy-start | bytes 9220
  131.3 2.5 %copy-start.19 = (f32[768]{0:T(1024)S(1)}, f32[768]{0:T(1024)}, u32[]{:S(2)}) copy-start(f32[768]{0:T(1024)} %copy-done.18) | copy-start | bytes 9220
  131.3 2.5 %copy-start.21 = (f32[768]{0:T(1024)S(1)}, f32[768]{0:T(1024)}, u32[]{:S(2)}) copy-start(f32[768]{0:T(1024)} %copy-done.20) | copy-start | bytes 9220
  131.3 2.5 %copy-start.23 = (f32[768]{0:T(1024)S(1)}, f32[768]{0:T(1024)}, u32[]{:S(2)}) copy-start(f32[768]{0:T(1024)} %copy-done.22) | copy-start | bytes 9220
  131.3 2.5 %copy-start.32 = (bf16[8,96,576]{2,1,0:T(8,128)(2,1)S(1)}, bf16[8,96,576]{2,1,0:T(8,128)(2,1)}, u32[]{:S(2)}) copy-start(bf16[8,96,576]{2,1,0:T(8,128)(2,1)} %get-tuple-element.38) | copy-start | bytes 2654212
  137.6 3.3 %copy-start.35 = (bf16[512,768]{1,0:T(8,128)(2,1)S(1)}, bf16[512,768]{1,0:T(8,128)(2,1)}, u32[]{:S(2)}) copy-start(bf16[512,768]{1,0:T(8,128)(2,1)} %copy-done.34) | copy-start | bytes 2359300
  140.9 1.8 copy-start.5
  149.0 38.8 %copy-start.27 = (f32[128]{0:T(128)S(1)}, f32[128]{0:T(128)}, u32[]{:S(2)}) copy-start(f32[128]{0:T(128)} %copy-done.26) | copy-start | bytes 1540
  149.1 38.8 %copy-start.29 = (f32[128]{0:T(128)S(1)}, f32[128]{0:T(128)}, u32[]{:S(2)}) copy-start(f32[128]{0:T(128)} %copy-done.28) | copy-start | bytes 1540
  186.3 1.7 copy-start.25
  186.4 1.8 copy-start.6
  188.1 1.1 copy-start.12
  188.2 1.7 copy-start.10
  209.3 1.1 copy-start.15
  209.3 1.7 copy-start.11
  210.4 3.6 %copy-start.9 = (f32[96,768]{1,0:T(8,128)S(1)}, f32[96,768]{1,0:T(8,128)}, u32[]{:S(2)}) copy-start(f32[96,768]{1,0:T(8,128)} %get-tuple-element.161) | copy-start | bytes 884740
  210.4 4.3 %copy-start.8 = (f32[96,768]{1,0:T(8,128)S(1)}, f32[96,768]{1,0:T(8,128)}, u32[]{:S(2)}) copy-start(f32[96,768]{1,0:T(8,128)} %get-tuple-element.163) | copy-start | bytes 884740
  212.9 2.5 %copy-start.30 = (f32[96]{0:T(128)}, f32[96]{0:T(128)S(1)}, u32[]{:S(2)}) copy-start(f32[96]{0:T(128)S(1)} %get-tuple-element.156) | copy-start | bytes 1156
